TPU v7x, 32 devices: a whole 2x2x4 slice. The times are simulated.
32 devices in a mesh: rep: 8 (over y, x, core), shard: 4 (over z).
Axes of the slice: x: 2, y: 2, z: 4, core: 2. Of those that a mesh axis runs over, the one named last changes fastest.
Arguments:
- inputs: bfloat16 [2, 32, 1024, 768], P(None, None, ('rep', 'shard')), may hold values from -6 to 6
- cotangent: bfloat16 [2, 32, 1024, 768], P(None, ('rep', 'shard')), may hold values from -6 to 6
- lengths: int32 [2, 32], replicated, may hold values from 64 to 1024, as said below
- order: int32 [2, 32], replicated, may hold values from 0 to 31, each once within a row
- random_blocks: int32 [2, 32, 12, 16, 3], replicated, may hold values from 0 to 15
- w_qkv: bfloat16 [768, 2304], P('shard'), may hold values from -0.21875 to 0.21875
- bias_query: bfloat16 [768], P('shard'), may hold values from -3 to 3
- bias_value: bfloat16 [768], P('shard'), may hold values from -3 to 3
- w_out: bfloat16 [768, 768], P('shard'), may hold values from -3.5 to 3.5
- bias_out: bfloat16 [768], P('shard'), may hold values from -3 to 3
- gain_first: bfloat16 [768], P('shard'), may hold values from 0.25 to 1.75
- shift_first: bfloat16 [768], P('shard'), may hold values from -3 to 3
- w_up: bfloat16 [768, 3072], P('shard'), may hold values from -0.21875 to 0.21875
- bias_up: bfloat16 [3072], P('shard'), may hold values from -3 to 3
- w_down: bfloat16 [3072, 768], P('shard'), may hold values from -0.109375 to 0.109375
- bias_down: bfloat16 [768], P('shard'), may hold values from -3 to 3
- gain_second: bfloat16 [768], P('shard'), may hold values from 0.25 to 1.75
- shift_second: bfloat16 [768], P('shard'), may hold values from -3 to 3
Outputs:
- output: bfloat16 [2, 32, 1024, 768], P(None, None, ('rep', 'shard'))
- grad_input: bfloat16 [2, 32, 1024, 768], P(None, None, ('rep', 'shard'))
- grad_w_qkv: float32 [768, 2304], P('shard')
- grad_bias_query: float32 [768], P('shard')
- grad_bias_value: float32 [768], P('shard')
- grad_w_out: float32 [768, 768], P('shard')
- grad_bias_out: float32 [768], P('shard')
- grad_gain_first: float32 [768], P('shard')
- grad_shift_first: float32 [768], P('shard')
- grad_w_up: float32 [768, 3072], P('shard')
- grad_bias_up: float32 [3072], P('shard')
- grad_w_down: float32 [3072, 768], P('shard')
- grad_bias_down: float32 [768], P('shard')
- grad_gain_second: float32 [768], P('shard')
- grad_shift_second: float32 [768], P('shard')
Inputs may be any that keep to these rules, and one draw needn't show every extreme that they name: `lengths`: in each micro-batch some sequence has 1024 tokens. `order`: each row is a permutation of the sequences of the micro-batch.
All inputs are finite; a program needn't handle non-finite values.
Results may differ from a plain program's by a relative error of at most 0.018.
Values may be sent and summed in bfloat16 or wider, within the bound.
No kernel may reach another device: no remote copies, remote signals or barrier semaphores. Data moves between devices by JAX's collectives and lax.ppermute only.
A program may use at most 320 MiB of HBM per device.

v0:
```python
import jax
import jax.numpy as jnp
from jax import lax
from jax.sharding import PartitionSpec as P

D = 768
HEADS = 12
HD = 64
BLOCK = 64
LEN = 1024


epsilon = 1e-06
masked_score = -1e30


def layer_norm(hidden, norm_gain, norm_shift):
    center = hidden - jnp.mean(hidden, axis=-1, keepdims=True)
    spread = jnp.mean(center * center, axis=-1, keepdims=True)
    return center * lax.rsqrt(spread + epsilon) * norm_gain + norm_shift


def exact_gelu(values):
    return jax.nn.gelu(values, approximate=False)


def block_table(chosen):
    block_count = chosen.shape[1]
    query_block = jnp.arange(block_count, dtype=jnp.int32)[:, None]
    key_block = jnp.arange(block_count, dtype=jnp.int32)[None, :]
    last_block = block_count - 1
    global_rows = (query_block == 0) | (query_block == last_block)
    global_cols = (key_block == 0) | (key_block == last_block)
    fixed_blocks = global_rows | global_cols | (jnp.abs(query_block - key_block) <= 1)
    picked = jnp.any(chosen[:, :, :, None] == key_block[None, None, :, :], axis=2)
    return fixed_blocks[None, :, :] | picked


def block_rows(allowed_table, row_start, row_count, length):
    head_count = allowed_table.shape[0]
    block_count = allowed_table.shape[2]
    table_rows = allowed_table[:, row_start // BLOCK : (row_start + row_count) // BLOCK]
    spread_mask = jnp.broadcast_to(
        table_rows[:, :, None, :, None], (head_count, row_count // BLOCK, BLOCK, block_count, BLOCK)
    )
    spread_mask = spread_mask.reshape(head_count, row_count, block_count * BLOCK)
    live_keys = jnp.arange(block_count * BLOCK, dtype=jnp.int32) < length
    return spread_mask & live_keys[None, None, :]


def product_left(left_rows, right_rows):
    return lax.dot_general(
        left_rows, right_rows, (((0,), (0,)), ((), ())), preferred_element_type=jnp.float32
    )


def product_right(left_rows, right_rows):
    return lax.dot_general(
        left_rows, right_rows, (((1,), (1,)), ((), ())), preferred_element_type=jnp.float32
    )


def split_heads(projected):
    return (
        projected[:, :D].reshape(LEN, HEADS, HD),
        projected[:, D : 2 * D].reshape(LEN, HEADS, HD),
        projected[:, 2 * D :].reshape(LEN, HEADS, HD),
    )


def attend_forward(projected, allowed_table, length):
    row_count = min(512, LEN)
    scale = HD ** (-0.5)
    queries, key_heads, value_heads = split_heads(projected)
    contexts = []
    totals = []
    for row_start in range(0, LEN, row_count):
        allowed = block_rows(allowed_table, row_start, row_count, length)
        raw_scores = jnp.einsum(
            "qhd,khd->hqk",
            queries[row_start : row_start + row_count],
            key_heads,
            preferred_element_type=jnp.float32,
        )
        scores = jnp.where(allowed, scale * raw_scores, masked_score)
        top_score = jnp.max(scores, axis=-1, keepdims=True)
        shifted = jnp.exp(scores - top_score)
        summed = jnp.sum(shifted, axis=-1, keepdims=True)
        weights = (shifted / summed).astype(jnp.bfloat16)
        context = jnp.einsum(
            "hqk,khd->qhd", weights, value_heads, preferred_element_type=jnp.float32
        )
        live_rows = row_start + jnp.arange(row_count, dtype=jnp.int32) < length
        contexts.append(context.reshape(row_count, D) * live_rows[:, None].astype(jnp.float32))
        totals.append(top_score + jnp.log(summed))
    return (jnp.concatenate(contexts, axis=0), jnp.concatenate(totals, axis=1))


def attend_backward(projected, allowed_table, length, totals, grad_context):
    row_count = min(512, LEN)
    scale = HD ** (-0.5)
    queries, key_heads, value_heads = split_heads(projected)
    grad_heads = grad_context.reshape(LEN, HEADS, HD)
    grad_queries = []
    grad_keys = jnp.zeros((LEN, HEADS, HD), jnp.float32)
    grad_values = jnp.zeros((LEN, HEADS, HD), jnp.float32)
    for row_start in range(0, LEN, row_count):
        block_queries = queries[row_start : row_start + row_count]
        block_grads = grad_heads[row_start : row_start + row_count]
        allowed = block_rows(allowed_table, row_start, row_count, length)
        raw_scores = jnp.einsum(
            "qhd,khd->hqk", block_queries, key_heads, preferred_element_type=jnp.float32
        )
        scores = jnp.where(allowed, scale * raw_scores, masked_score)
        weights = jnp.exp(scores - totals[:, row_start : row_start + row_count])
        grad_weights = jnp.einsum(
            "qhd,khd->hqk", block_grads, value_heads, preferred_element_type=jnp.float32
        )
        grad_values = grad_values + jnp.einsum(
            "hqk,qhd->khd",
            weights.astype(jnp.bfloat16),
            block_grads,
            preferred_element_type=jnp.float32,
        )
        inner_sum = jnp.sum(weights * grad_weights, axis=-1, keepdims=True)
        grad_scores = (scale * (weights * (grad_weights - inner_sum))).astype(jnp.bfloat16)
        grad_queries.append(
            jnp.einsum(
                "hqk,khd->qhd", grad_scores, key_heads, preferred_element_type=jnp.float32
            ).reshape(row_count, D)
        )
        grad_keys = grad_keys + jnp.einsum(
            "hqk,qhd->khd", grad_scores, block_queries, preferred_element_type=jnp.float32
        )
    return jnp.concatenate(
        [
            jnp.concatenate(grad_queries, axis=0),
            grad_keys.reshape(LEN, D),
            grad_values.reshape(LEN, D),
        ],
        axis=1,
    )


def per_device(
    inputs,
    cotangent,
    lengths,
    order,
    random_blocks,
    w_qkv,
    bias_query,
    bias_value,
    w_out,
    bias_out,
    gain_first,
    shift_first,
    w_up,
    bias_up,
    w_down,
    bias_down,
    gain_second,
    shift_second,
):
    device = lax.axis_index(("rep", "shard"))
    group_size = lax.axis_size("shard")
    params = (
        w_qkv,
        bias_query,
        bias_value,
        w_out,
        bias_out,
        gain_first,
        shift_first,
        w_up,
        bias_up,
        w_down,
        bias_down,
        gain_second,
        shift_second,
    )

    def step(grad_sums, batch_items):
        batch_inputs, batch_cotangent, batch_lengths, batch_order, batch_blocks = batch_items
        source = batch_order[device]
        length = batch_lengths[source]
        allowed_table = block_table(
            lax.dynamic_index_in_dim(batch_blocks, source, 0, keepdims=False)
        )
        sorted_rows = jnp.take(batch_inputs, batch_order, axis=0)
        arrived = lax.all_to_all(
            sorted_rows, ("rep", "shard"), split_axis=0, concat_axis=1, tiled=True
        )[0]
        gathered = (
            lax.all_gather(w_qkv, "shard", axis=0, tiled=True),
            lax.all_gather(bias_query, "shard", axis=0, tiled=True),
            lax.all_gather(bias_value, "shard", axis=0, tiled=True),
            lax.all_gather(w_out, "shard", axis=0, tiled=True),
            lax.all_gather(bias_out, "shard", axis=0, tiled=True),
            lax.all_gather(gain_first, "shard", axis=0, tiled=True),
            lax.all_gather(shift_first, "shard", axis=0, tiled=True),
            lax.all_gather(w_up, "shard", axis=0, tiled=True),
            lax.all_gather(bias_up, "shard", axis=0, tiled=True),
            lax.all_gather(w_down, "shard", axis=0, tiled=True),
            lax.all_gather(bias_down, "shard", axis=0, tiled=True),
            lax.all_gather(gain_second, "shard", axis=0, tiled=True),
            lax.all_gather(shift_second, "shard", axis=0, tiled=True),
        )
        (
            proj_weight,
            query_bias,
            value_bias,
            out_weight,
            out_bias,
            norm_gain,
            norm_shift,
            lift_weight,
            lift_bias,
            drop_weight,
            drop_bias,
            final_gain,
            final_shift,
        ) = gathered
        tokens = arrived.astype(jnp.float32)
        bias_all = jnp.concatenate([query_bias, jnp.zeros_like(query_bias), value_bias]).astype(
            jnp.float32
        )
        projected = (
            jnp.dot(arrived, proj_weight, preferred_element_type=jnp.float32) + bias_all
        ).astype(jnp.bfloat16)
        context, totals = attend_forward(projected, allowed_table, length)
        context_low = context.astype(jnp.bfloat16)
        attn_mixed = jnp.dot(
            context_low, out_weight, preferred_element_type=jnp.float32
        ) + out_bias.astype(jnp.float32)
        normed, norm_pull = jax.vjp(
            layer_norm,
            tokens + attn_mixed,
            norm_gain.astype(jnp.float32),
            norm_shift.astype(jnp.float32),
        )
        normed_low = normed.astype(jnp.bfloat16)
        lifted = jnp.dot(
            normed_low, lift_weight, preferred_element_type=jnp.float32
        ) + lift_bias.astype(jnp.float32)
        activated, gelu_pull = jax.vjp(exact_gelu, lifted)
        activated_low = activated.astype(jnp.bfloat16)
        lowered = jnp.dot(
            activated_low, drop_weight, preferred_element_type=jnp.float32
        ) + drop_bias.astype(jnp.float32)
        result, final_pull = jax.vjp(
            layer_norm,
            normed + lowered,
            final_gain.astype(jnp.float32),
            final_shift.astype(jnp.float32),
        )
        back_weights = (
            lax.all_gather(w_qkv, "shard", axis=0, tiled=True),
            lax.all_gather(bias_query, "shard", axis=0, tiled=True),
            lax.all_gather(bias_value, "shard", axis=0, tiled=True),
            lax.all_gather(w_out, "shard", axis=0, tiled=True),
            lax.all_gather(bias_out, "shard", axis=0, tiled=True),
            lax.all_gather(gain_first, "shard", axis=0, tiled=True),
            lax.all_gather(shift_first, "shard", axis=0, tiled=True),
            lax.all_gather(w_up, "shard", axis=0, tiled=True),
            lax.all_gather(bias_up, "shard", axis=0, tiled=True),
            lax.all_gather(w_down, "shard", axis=0, tiled=True),
            lax.all_gather(bias_down, "shard", axis=0, tiled=True),
            lax.all_gather(gain_second, "shard", axis=0, tiled=True),
            lax.all_gather(shift_second, "shard", axis=0, tiled=True),
        )
        proj_back = back_weights[0]
        out_back = back_weights[3]
        lift_back = back_weights[7]
        drop_back = back_weights[9]
        grad_second, grad_final_gain, grad_final_shift = final_pull(
            batch_cotangent[0].astype(jnp.float32)
        )
        grad_drop_bias = jnp.sum(grad_second, axis=0)
        grad_second_low = grad_second.astype(jnp.bfloat16)
        grad_drop_weight = product_left(activated_low, grad_second_low)
        grad_lifted = gelu_pull(product_right(grad_second_low, drop_back))[0]
        grad_lift_bias = jnp.sum(grad_lifted, axis=0)
        grad_lifted_low = grad_lifted.astype(jnp.bfloat16)
        grad_lift_weight = product_left(normed_low, grad_lifted_low)
        grad_normed = grad_second + product_right(grad_lifted_low, lift_back)
        grad_first, grad_norm_gain, grad_norm_shift = norm_pull(grad_normed)
        grad_out_bias = jnp.sum(grad_first, axis=0)
        grad_first_low = grad_first.astype(jnp.bfloat16)
        grad_out_weight = product_left(context_low, grad_first_low)
        live_rows = (jnp.arange(LEN, dtype=jnp.int32) < length)[:, None]
        grad_context = jnp.where(
            live_rows,
            product_right(grad_first_low, out_back).astype(jnp.bfloat16),
            jnp.zeros((), jnp.bfloat16),
        )
        grad_projected = attend_backward(projected, allowed_table, length, totals, grad_context)
        grad_projected_low = grad_projected.astype(jnp.bfloat16)
        grad_proj_weight = product_left(arrived, grad_projected_low)
        grad_tokens = (grad_first + product_right(grad_projected_low, proj_back)).astype(
            jnp.bfloat16
        )
        new_terms = (
            grad_proj_weight,
            jnp.sum(grad_projected[:, :D], axis=0),
            jnp.sum(grad_projected[:, 2 * D :], axis=0),
            grad_out_weight,
            grad_out_bias,
            grad_norm_gain,
            grad_norm_shift,
            grad_lift_weight,
            grad_lift_bias,
            grad_drop_weight,
            grad_drop_bias,
            grad_final_gain,
            grad_final_shift,
        )
        grad_sums = tuple((running + new_term for running, new_term in zip(grad_sums, new_terms)))
        sent_output, sent_grads = (
            lax.all_to_all(
                result.astype(jnp.bfloat16)[None],
                ("rep", "shard"),
                split_axis=1,
                concat_axis=0,
                tiled=True,
            ),
            lax.all_to_all(
                grad_tokens[None], ("rep", "shard"), split_axis=1, concat_axis=0, tiled=True
            ),
        )
        inverse = jnp.argsort(batch_order)
        return (
            grad_sums,
            (jnp.take(sent_output, inverse, axis=0), jnp.take(sent_grads, inverse, axis=0)),
        )

    zeros = tuple(
        (
            jnp.zeros((param.shape[0] * group_size,) + param.shape[1:], jnp.float32)
            for param in params
        )
    )
    grad_sums, (outputs, grad_inputs) = lax.scan(
        step, zeros, (inputs, cotangent, lengths, order, random_blocks)
    )
    owned = (
        lax.psum_scatter(grad_sums[0], "shard", scatter_dimension=0, tiled=True),
        lax.psum_scatter(grad_sums[1], "shard", scatter_dimension=0, tiled=True),
        lax.psum_scatter(grad_sums[2], "shard", scatter_dimension=0, tiled=True),
        lax.psum_scatter(grad_sums[3], "shard", scatter_dimension=0, tiled=True),
        lax.psum_scatter(grad_sums[4], "shard", scatter_dimension=0, tiled=True),
        lax.psum_scatter(grad_sums[5], "shard", scatter_dimension=0, tiled=True),
        lax.psum_scatter(grad_sums[6], "shard", scatter_dimension=0, tiled=True),
        lax.psum_scatter(grad_sums[7], "shard", scatter_dimension=0, tiled=True),
        lax.psum_scatter(grad_sums[8], "shard", scatter_dimension=0, tiled=True),
        lax.psum_scatter(grad_sums[9], "shard", scatter_dimension=0, tiled=True),
        lax.psum_scatter(grad_sums[10], "shard", scatter_dimension=0, tiled=True),
        lax.psum_scatter(grad_sums[11], "shard", scatter_dimension=0, tiled=True),
        lax.psum_scatter(grad_sums[12], "shard", scatter_dimension=0, tiled=True),
    )
    summed = (
        lax.psum(owned[0].astype(jnp.bfloat16), "rep").astype(jnp.float32),
        lax.psum(owned[1].astype(jnp.bfloat16), "rep").astype(jnp.float32),
        lax.psum(owned[2].astype(jnp.bfloat16), "rep").astype(jnp.float32),
        lax.psum(owned[3].astype(jnp.bfloat16), "rep").astype(jnp.float32),
        lax.psum(owned[4].astype(jnp.bfloat16), "rep").astype(jnp.float32),
        lax.psum(owned[5].astype(jnp.bfloat16), "rep").astype(jnp.float32),
        lax.psum(owned[6].astype(jnp.bfloat16), "rep").astype(jnp.float32),
        lax.psum(owned[7].astype(jnp.bfloat16), "rep").astype(jnp.float32),
        lax.psum(owned[8].astype(jnp.bfloat16), "rep").astype(jnp.float32),
        lax.psum(owned[9].astype(jnp.bfloat16), "rep").astype(jnp.float32),
        lax.psum(owned[10].astype(jnp.bfloat16), "rep").astype(jnp.float32),
        lax.psum(owned[11].astype(jnp.bfloat16), "rep").astype(jnp.float32),
        lax.psum(owned[12].astype(jnp.bfloat16), "rep").astype(jnp.float32),
    )
    return (
        outputs,
        grad_inputs,
        summed[0],
        summed[1],
        summed[2],
        summed[3],
        summed[4],
        summed[5],
        summed[6],
        summed[7],
        summed[8],
        summed[9],
        summed[10],
        summed[11],
        summed[12],
    )


def solution(mesh):
    placed = (
        P(None, None, ("rep", "shard"), None),
        P(None, ("rep", "shard"), None, None),
        P(),
        P(),
        P(),
        P("shard", None),
        P("shard"),
        P("shard"),
        P("shard", None),
        P("shard"),
        P("shard"),
        P("shard"),
        P("shard", None),
        P("shard"),
        P("shard", None),
        P("shard"),
        P("shard"),
        P("shard"),
    )
    return jax.shard_map(
        per_device,
        mesh=mesh,
        in_specs=placed,
        out_specs=(
            P(None, None, ("rep", "shard"), None),
            P(None, None, ("rep", "shard"), None),
            P("shard", None),
            P("shard"),
            P("shard"),
            P("shard", None),
            P("shard"),
            P("shard"),
            P("shard"),
            P("shard", None),
            P("shard"),
            P("shard", None),
            P("shard"),
            P("shard"),
            P("shard"),
        ),
        check_vma=False,
    )
```

profile of v0, /device:TPU:0, one launch (start us, length us, event | category | flops | bytes accessed | tf_op | source)
XLA Modules:
  0.0 2151.5 jit_solution(8109268617792567564)
XLA Ops:
  11.0 1539.7 %while.42 = (s32[]{:T(128)}, f32[768,2304]{1,0:T(8,128)}, f32[768]{0:T(1024)}, f32[768]{0:T(1024)}, f32[768,768]{1,0:T(8,128)}, /*index=5*/f32[768]{0:T(1024)}, ...) while((s32[]{:T(128)}, f32[768,2304]{1,0:T(8,128)}, ...), condition=%wide.region_27.29_spmd.clone, body=%wide.region_0.28_spmd.clone.sunk | while | flops 53860462592 | bytes 1168448128 | solution.py:343
  32.1 82.0 %all-reduce.30 = (bf16[768]{0:T(1024)(128)(2,1)S(1)}, bf16[768]{0:T(1024)(128)(2,1)S(1)}, bf16[768]{0:T(1024)(128)(2,1)S(1)}, bf16[768]{0:T(1024)(128)(2,1)S(1)}...) all-reduce(bf16[768]{0:T(1024)(128)(2,1)S(1)} %dynamic-update-slice, ...), channel_id=1, replica_groups=mesh['rep'=8,'shard'=4] {'shard'}, use_global_device_ids=true, to_apply=%add.3 | all-reduce | flops 6144 | bytes 24576 | tf_op jit(solution)/shard_map/while
  141.7 33.2 %reshape.500 = pred[12,512,1024]{2,1,0:T(32,128)(4,1)} reshape(pred[12,8,64,16,64]{4,3,2,1,0:T(8,128)(4,1)} %broadcast_in_dim.257) | data formatting | bytes 12582912 | tf_op jit(solution)/shard_map/while/body/eval_jaxpr/reshape | solution.py:46
  180.1 33.1 %reshape.501 = pred[12,512,1024]{2,1,0:T(32,128)(4,1)} reshape(pred[12,8,64,16,64]{4,3,2,1,0:T(8,128)(4,1)} %broadcast_in_dim.258) | data formatting | bytes 12582912 | tf_op jit(solution)/shard_map/while/body/eval_jaxpr/reshape | solution.py:46
  315.1 38.2 %multiply_convert_fusion.4 = (bf16[1024,3072]{1,0:T(8,128)(2,1)}, f32[1024,3072]{1,0:T(8,128)}, f32[1024,3072]{1,0:T(8,128)}) fusion(f32[3072]{0:T(1024)S(1)} %bitcast.266, bf16[768,3072]{1,0:T(8,128)(2,1)} %all-gather.13.cloned.1.call-done, f32[1024,768]{0,1:T(8,128)S(1)} %get-tuple-element.1268, f32[768]{0:T(1024)S(1)} %convert_element_type.495, ...), kind=kOutput, calls=%fused_computation.30.clone.1 | convolution fusion | flops 5043388416 | bytes 39348224 | tf_op jit(solution)/shard_map/while/body/eval_jaxpr/dot_general | solution.py:243
  413.8 45.7 %fusion.259 = f32[12,64,1024]{2,1,0:T(8,128)} fusion(bf16[512,12,64]{0,2,1:T(8,128)(2,1)} %bitcast.263, f32[12,512,1024]{2,1,0:T(8,128)} %fusion.258, f32[12,512,1024]{2,1,0:T(8,128)} %get-tuple-element.1266, f32[12,512]{1,0:T(8,128)S(1)} %copy-done.19), kind=kOutput, calls=%fused_computation.48.clone.1 | convolution fusion | flops 849353728 | bytes 54288384 | tf_op jit(solution)/shard_map/while/body/eval_jaxpr/hqk,qhd->khd/dot_general | solution.py:132
  459.5 51.1 %bitcast_convert_fusion.8 = (bf16[512,12,64]{0,2,1:T(8,128)(2,1)}, f32[12,64,512]{2,1,0:T(8,128)}) fusion(bf16[1024,12,64]{0,2,1:T(8,128)(2,1)S(1)} %bitcast.245, f32[12,512,1024]{2,1,0:T(8,128)} %fusion.258, f32[12,512,1024]{2,1,0:T(8,128)} %get-tuple-element.1266, f32[12,512]{1,0:T(8,128)S(1)} %copy-done.19), kind=kOutput, calls=%fused_computation.102.clone.1 | convolution fusion | flops 849746944 | bytes 54288384 | tf_op jit(solution)/shard_map/while/body/eval_jaxpr/hqk,khd->qhd/dot_general | solution.py:128
  567.5 51.2 %bitcast_convert_fusion.7 = (bf16[512,12,64]{0,2,1:T(8,128)(2,1)}, f32[12,64,512]{2,1,0:T(8,128)}) fusion(bf16[1024,12,64]{0,2,1:T(8,128)(2,1)S(1)} %bitcast.246, f32[12,512,1024]{2,1,0:T(8,128)} %fusion.260, f32[12,512,1024]{2,1,0:T(8,128)} %get-tuple-element.1262, f32[12,512]{1,0:T(8,128)S(1)} %copy-done.20), kind=kOutput, calls=%fused_computation.100.clone.1 | convolution fusion | flops 849746944 | bytes 54288384 | tf_op jit(solution)/shard_map/while/body/eval_jaxpr/hqk,khd->qhd/dot_general | solution.py:128
  618.8 46.2 %add_convert_fusion.19 = bf16[12,64,1024]{2,1,0:T(8,128)(2,1)} fusion(f32[12,64,1024]{2,1,0:T(8,128)} %fusion.259, bf16[512,12,64]{0,2,1:T(8,128)(2,1)} %bitcast.261, f32[12,512,1024]{2,1,0:T(8,128)} %fusion.260, f32[12,512,1024]{2,1,0:T(8,128)} %get-tuple-element.1262, f32[12,512]{1,0:T(8,128)S(1)} %copy-done.20), kind=kOutput, calls=%fused_computation.72.clone.1 | convolution fusion | flops 850926592 | bytes 55861248 | tf_op jit(solution)/shard_map/while/body/eval_jaxpr/hqk,qhd->khd/dot_general | solution.py:132
  798.2 81.9 %all-reduce.30 = (bf16[768]{0:T(1024)(128)(2,1)S(1)}, bf16[768]{0:T(1024)(128)(2,1)S(1)}, bf16[768]{0:T(1024)(128)(2,1)S(1)}, bf16[768]{0:T(1024)(128)(2,1)S(1)}...) all-reduce(bf16[768]{0:T(1024)(128)(2,1)S(1)} %dynamic-update-slice, ...), channel_id=1, replica_groups=mesh['rep'=8,'shard'=4] {'shard'}, use_global_device_ids=true, to_apply=%add.3 | all-reduce | flops 6144 | bytes 24576 | tf_op jit(solution)/shard_map/while
  907.1 33.2 %reshape.500 = pred[12,512,1024]{2,1,0:T(32,128)(4,1)} reshape(pred[12,8,64,16,64]{4,3,2,1,0:T(8,128)(4,1)} %broadcast_in_dim.257) | data formatting | bytes 12582912 | tf_op jit(solution)/shard_map/while/body/eval_jaxpr/reshape | solution.py:46
  945.5 33.1 %reshape.501 = pred[12,512,1024]{2,1,0:T(32,128)(4,1)} reshape(pred[12,8,64,16,64]{4,3,2,1,0:T(8,128)(4,1)} %broadcast_in_dim.258) | data formatting | bytes 12582912 | tf_op jit(solution)/shard_map/while/body/eval_jaxpr/reshape | solution.py:46
  1080.5 38.2 %multiply_convert_fusion.4 = (bf16[1024,3072]{1,0:T(8,128)(2,1)}, f32[1024,3072]{1,0:T(8,128)}, f32[1024,3072]{1,0:T(8,128)}) fusion(f32[3072]{0:T(1024)S(1)} %bitcast.266, bf16[768,3072]{1,0:T(8,128)(2,1)} %all-gather.13.cloned.1.call-done, f32[1024,768]{0,1:T(8,128)S(1)} %get-tuple-element.1268, f32[768]{0:T(1024)S(1)} %convert_element_type.495, ...), kind=kOutput, calls=%fused_computation.30.clone.1 | convolution fusion | flops 5043388416 | bytes 39348224 | tf_op jit(solution)/shard_map/while/body/eval_jaxpr/dot_general | solution.py:243
  1135.3 18.8 fusion.254
  1179.1 45.7 %fusion.259 = f32[12,64,1024]{2,1,0:T(8,128)} fusion(bf16[512,12,64]{0,2,1:T(8,128)(2,1)} %bitcast.263, f32[12,512,1024]{2,1,0:T(8,128)} %fusion.258, f32[12,512,1024]{2,1,0:T(8,128)} %get-tuple-element.1266, f32[12,512]{1,0:T(8,128)S(1)} %copy-done.19), kind=kOutput, calls=%fused_computation.48.clone.1 | convolution fusion | flops 849353728 | bytes 54288384 | tf_op jit(solution)/shard_map/while/body/eval_jaxpr/hqk,qhd->khd/dot_general | solution.py:132
  1224.8 51.2 %bitcast_convert_fusion.8 = (bf16[512,12,64]{0,2,1:T(8,128)(2,1)}, f32[12,64,512]{2,1,0:T(8,128)}) fusion(bf16[1024,12,64]{0,2,1:T(8,128)(2,1)S(1)} %bitcast.245, f32[12,512,1024]{2,1,0:T(8,128)} %fusion.258, f32[12,512,1024]{2,1,0:T(8,128)} %get-tuple-element.1266, f32[12,512]{1,0:T(8,128)S(1)} %copy-done.19), kind=kOutput, calls=%fused_computation.102.clone.1 | convolution fusion | flops 849746944 | bytes 54288384 | tf_op jit(solution)/shard_map/while/body/eval_jaxpr/hqk,khd->qhd/dot_general | solution.py:128
  1332.8 51.2 %bitcast_convert_fusion.7 = (bf16[512,12,64]{0,2,1:T(8,128)(2,1)}, f32[12,64,512]{2,1,0:T(8,128)}) fusion(bf16[1024,12,64]{0,2,1:T(8,128)(2,1)S(1)} %bitcast.246, f32[12,512,1024]{2,1,0:T(8,128)} %fusion.260, f32[12,512,1024]{2,1,0:T(8,128)} %get-tuple-element.1262, f32[12,512]{1,0:T(8,128)S(1)} %copy-done.20), kind=kOutput, calls=%fused_computation.100.clone.1 | convolution fusion | flops 849746944 | bytes 54288384 | tf_op jit(solution)/shard_map/while/body/eval_jaxpr/hqk,khd->qhd/dot_general | solution.py:128
  1384.0 46.2 %add_convert_fusion.19 = bf16[12,64,1024]{2,1,0:T(8,128)(2,1)} fusion(f32[12,64,1024]{2,1,0:T(8,128)} %fusion.259, bf16[512,12,64]{0,2,1:T(8,128)(2,1)} %bitcast.261, f32[12,512,1024]{2,1,0:T(8,128)} %fusion.260, f32[12,512,1024]{2,1,0:T(8,128)} %get-tuple-element.1262, f32[12,512]{1,0:T(8,128)S(1)} %copy-done.20), kind=kOutput, calls=%fused_computation.72.clone.1 | convolution fusion | flops 850926592 | bytes 55861248 | tf_op jit(solution)/shard_map/while/body/eval_jaxpr/hqk,qhd->khd/dot_general | solution.py:132
  1553.2 48.7 %reduce-scatter.7.cloned.1.call-done = f32[192,768]{1,0:T(8,128)} async-done(((f32[768,768]{1,0:T(8,128)}), f32[192,768]{1,0:T(8,128)}) %reduce-scatter.7.cloned.1.call-update) | async-done | bytes 589840 | tf_op jit(solution)/shard_map/reduce_scatter | solution.py:350
  1603.7 123.2 %reduce-scatter.5.cloned.1.call-done = f32[192,2304]{1,0:T(8,128)} async-done(((f32[768,2304]{1,0:T(8,128)}), f32[192,2304]{1,0:T(8,128)}) %reduce-scatter.5.cloned.1.call-update) | async-done | bytes 1769488 | tf_op jit(solution)/shard_map/reduce_scatter | solution.py:347
  1729.4 161.4 %reduce-scatter.9.cloned.1.call-done = f32[192,3072]{1,0:T(8,128)} async-done(((f32[768,3072]{1,0:T(8,128)}), f32[192,3072]{1,0:T(8,128)}) %reduce-scatter.9.cloned.1.call-update) | async-done | bytes 2359312 | tf_op jit(solution)/shard_map/reduce_scatter | solution.py:354
  1893.6 161.6 %reduce-scatter.11.cloned.1.call-done = f32[768,768]{1,0:T(8,128)} async-done(((f32[3072,768]{1,0:T(8,128)}), f32[768,768]{1,0:T(8,128)}) %reduce-scatter.11.cloned.1.call-update) | async-done | bytes 2359312 | tf_op jit(solution)/shard_map/reduce_scatter | solution.py:356
  2060.1 19.1 all-reduce.26
  2097.1 37.6 %all-reduce.33.cloned.1.call-done = (bf16[192,2304]{1,0:T(8,128)(2,1)}, bf16[192,768]{1,0:T(8,128)(2,1)}, bf16[192,3072]{1,0:T(8,128)(2,1)}, bf16[768,768]{1,0:T(8,128)(2,1)}) async-done(((bf16[192,2304]{1,0:T(8,128)(2,1)}, bf16[192,768]{1,0:T(8,128)(2,1)}, bf16[192,3072]{1,0:T(8,128)(2,1)}, bf16[768,768]{1,0:T(8,128)(2,1)}), (bf16[192,2304]{1,0:T(8,128)(2,1)}, bf16[192,768]{1,0:T(8,128)(2,1)}, ...) | async-done | bytes 3538960 | tf_op jit(solution)/shard_map/psum | solution.py:362
  (627 shorter events, 791.9 us)
Async XLA Ops:
  11.0 207.3 %all-gather.11.cloned.1.call-start = ((), (), s32[]{:S(2)}) async-start(), calls=%async_computation.13 | async-start | bytes 4423680 | tf_op jit(solution)/shard_map/while/body/eval_jaxpr/all_gather | solution.py:195
  11.7 299.1 %all-gather.9.cloned.1.call-start = ((), (), s32[]{:S(2)}) async-start(), calls=%async_computation.12 | async-start | bytes 1474560 | tf_op jit(solution)/shard_map/while/body/eval_jaxpr/all_gather | solution.py:198
  12.4 302.7 %all-gather.13.cloned.1.call-start = ((), (), s32[]{:S(2)}) async-start(), calls=%async_computation.14 | async-start | bytes 5898240 | tf_op jit(solution)/shard_map/while/body/eval_jaxpr/all_gather | solution.py:202
  17.6 199.0 %all-to-all-start = ((bf16[32,32,768]{2,1,0:T(8,128)(2,1)}), bf16[32,32,768]{2,1,0:T(8,128)(2,1)S(1)}, u32[]{:S(2)}, u32[]{:S(2)}) async-start(bf16[32,32,768]{2,1,0:T(8,128)(2,1)} %broadcast_select_fusion.4), calls=%async_computation | async-start | bytes 3145728 | tf_op jit(solution)/shard_map/while/body/eval_jaxpr/all_to_all | solution.py:191
  24.9 328.4 %all-gather.15.cloned.1.call-start = ((), (), s32[]{:S(2)}) async-start(), calls=%async_computation.15 | async-start | bytes 5898240 | tf_op jit(solution)/shard_map/while/body/eval_jaxpr/all_gather | solution.py:204
  563.9 156.6 %all-to-all-start.2 = ((bf16[32,2,12288]{2,1,0:T(2,128)(2,1)}), bf16[32,2,12288]{2,1,0:T(2,128)(2,1)}, u32[]{:S(2)}, u32[]{:S(2)}) async-start(bf16[32,2,12288]{2,1,0:T(2,128)(2,1)} %reshape.505), calls=%async_computation.2 | async-start | bytes 3145728 | tf_op jit(solution)/shard_map/while/body/eval_jaxpr/all_to_all | solution.py:320
  720.6 42.3 %all-to-all-start.1 = ((bf16[32,2,12288]{2,1,0:T(2,128)(2,1)}), bf16[32,2,12288]{2,1,0:T(2,128)(2,1)}, u32[]{:S(2)}, u32[]{:S(2)}) async-start(bf16[32,2,12288]{2,1,0:T(2,128)(2,1)} %reshape.503), calls=%async_computation.1 | async-start | bytes 3145728 | tf_op jit(solution)/shard_map/while/body/eval_jaxpr/all_to_all | solution.py:327
  779.7 204.0 %all-gather.11.cloned.1.call-start = ((), (), s32[]{:S(2)}) async-start(), calls=%async_computation.13 | async-start | bytes 4423680 | tf_op jit(solution)/shard_map/while/body/eval_jaxpr/all_gather | solution.py:195
  780.3 295.9 %all-gather.9.cloned.1.call-start = ((), (), s32[]{:S(2)}) async-start(), calls=%async_computation.12 | async-start | bytes 1474560 | tf_op jit(solution)/shard_map/while/body/eval_jaxpr/all_gather | solution.py:198
  780.9 299.6 %all-gather.13.cloned.1.call-start = ((), (), s32[]{:S(2)}) async-start(), calls=%async_computation.14 | async-start | bytes 5898240 | tf_op jit(solution)/shard_map/while/body/eval_jaxpr/all_gather | solution.py:202
  786.0 196.0 %all-to-all-start = ((bf16[32,32,768]{2,1,0:T(8,128)(2,1)}), bf16[32,32,768]{2,1,0:T(8,128)(2,1)S(1)}, u32[]{:S(2)}, u32[]{:S(2)}) async-start(bf16[32,32,768]{2,1,0:T(8,128)(2,1)} %broadcast_select_fusion.4), calls=%async_computation | async-start | bytes 3145728 | tf_op jit(solution)/shard_map/while/body/eval_jaxpr/all_to_all | solution.py:191
  790.7 327.9 %all-gather.15.cloned.1.call-start = ((), (), s32[]{:S(2)}) async-start(), calls=%async_computation.15 | async-start | bytes 5898240 | tf_op jit(solution)/shard_map/while/body/eval_jaxpr/all_gather | solution.py:204
  1329.2 160.3 %all-to-all-start.2 = ((bf16[32,2,12288]{2,1,0:T(2,128)(2,1)}), bf16[32,2,12288]{2,1,0:T(2,128)(2,1)}, u32[]{:S(2)}, u32[]{:S(2)}) async-start(bf16[32,2,12288]{2,1,0:T(2,128)(2,1)} %reshape.505), calls=%async_computation.2 | async-start | bytes 3145728 | tf_op jit(solution)/shard_map/while/body/eval_jaxpr/all_to_all | solution.py:320
  1489.5 42.1 %all-to-all-start.1 = ((bf16[32,2,12288]{2,1,0:T(2,128)(2,1)}), bf16[32,2,12288]{2,1,0:T(2,128)(2,1)}, u32[]{:S(2)}, u32[]{:S(2)}) async-start(bf16[32,2,12288]{2,1,0:T(2,128)(2,1)} %reshape.503), calls=%async_computation.1 | async-start | bytes 3145728 | tf_op jit(solution)/shard_map/while/body/eval_jaxpr/all_to_all | solution.py:327
  1550.7 51.2 %reduce-scatter.7.cloned.1.call-start = ((), (), s32[]{:S(2)}) async-start(), calls=%async_computation.8 | async-start | bytes 2949120 | tf_op jit(solution)/shard_map/reduce_scatter | solution.py:350
  1551.2 175.6 %reduce-scatter.5.cloned.1.call-start = ((), (), s32[]{:S(2)}) async-start(), calls=%async_computation.7 | async-start | bytes 8847360 | tf_op jit(solution)/shard_map/reduce_scatter | solution.py:347
  1551.8 339.0 %reduce-scatter.9.cloned.1.call-start = ((), (), s32[]{:S(2)}) async-start(), calls=%async_computation.9 | async-start | bytes 11796480 | tf_op jit(solution)/shard_map/reduce_scatter | solution.py:354
  1552.4 502.9 %reduce-scatter.11.cloned.1.call-start = ((), (), s32[]{:S(2)}) async-start(), calls=%async_computation.10 | async-start | bytes 11796480 | tf_op jit(solution)/shard_map/reduce_scatter | solution.py:356
  1553.2 581.6 %all-reduce.33.cloned.1.call-start = ((), (), s32[]{:S(2)}) async-start(), calls=%async_computation.11 | async-start | bytes 7077888 | tf_op jit(solution)/shard_map/psum | solution.py:362
  1729.3 330.7 %copy-start.39 = (f32[768]{0:T(1024)S(1)}, f32[768]{0:T(1024)}, u32[]{:S(2)}) copy-start(f32[768]{0:T(1024)} %get-tuple-element.560) | copy-start | bytes 9220
  1729.3 330.7 %copy-start.42 = (f32[768]{0:T(1024)S(1)}, f32[768]{0:T(1024)}, u32[]{:S(2)}) copy-start(f32[768]{0:T(1024)} %get-tuple-element.559) | copy-start | bytes 9220
  1729.4 330.7 %copy-start.45 = (f32[768]{0:T(1024)S(1)}, f32[768]{0:T(1024)}, u32[]{:S(2)}) copy-start(f32[768]{0:T(1024)} %get-tuple-element.558) | copy-start | bytes 9220
  1729.4 330.7 %copy-start.48 = (f32[768]{0:T(1024)S(1)}, f32[768]{0:T(1024)}, u32[]{:S(2)}) copy-start(f32[768]{0:T(1024)} %get-tuple-element.556) | copy-start | bytes 9220
  1729.4 330.7 %copy-start.51 = (f32[768]{0:T(1024)S(1)}, f32[768]{0:T(1024)}, u32[]{:S(2)}) copy-start(f32[768]{0:T(1024)} %get-tuple-element.555) | copy-start | bytes 9220
  (133 other events, 4338.4 us)
Sparse Core Ops, SparseCore 0:
  13.3 106.4 all-gather.10
  121.4 28.7 all-gather.8
  151.8 88.6 all-gather.12
  241.8 87.7 all-gather.14
  781.8 103.8 all-gather.10
  887.1 28.7 all-gather.8
  917.5 88.6 all-gather.12
  1007.7 87.7 all-gather.14
Sparse Core Ops, SparseCore 1:
  1554.0 47.8 reduce-scatter.6
  1604.0 122.7 reduce-scatter.4
  1729.1 161.7 reduce-scatter.8
  1893.2 162.0 reduce-scatter.10
  2060.1 74.5 all-reduce.32
where the time goes:
time: 2160 us; the launch traced here: 2150 us
  matrix products  846 us (39%)
  waiting for transfers between devices  559 us (26%)
  local copies, waits for them, and re-layouts  300 us (14%)
  blocking collectives  222 us (10%)
  other arithmetic  164 us (8%)
  starting transfers between devices  32.6 us (2%)
    dot_general x4, matrix products, attend_backward(): jnp.einsum('hqk,khd->qhd', grad_scores, key_heads, preferred_element_type...  205 us
    dot_general x4, matrix products, attend_backward(): jnp.einsum('hqk,qhd->khd', grad_scores, block_queries, preferred_element_...  184 us
    while x2, blocking collectives  164 us
    reduce_scatter x1, waiting for transfers between devices, per_device(): lax.psum_scatter(grad_sums[9], 'shard', scatter_dimension=0, tiled=True)  162 us
    reduce_scatter x1, waiting for transfers between devices, per_device(): lax.psum_scatter(grad_sums[7], 'shard', scatter_dimension=0, tiled=True)  161 us
    reshape x4, local copies, waits for them, and re-layouts, block_rows(): spread_mask.reshape(head_count, row_count, block_count * BLOCK)  133 us
    reduce_scatter x1, waiting for transfers between devices, per_device(): lax.psum_scatter(grad_sums[0], 'shard', scatter_dimension=0, tiled=True)  123 us
    dot_general x8, matrix products, product_right(): lax.dot_general(left_rows, right_rows, (((1,), (1,)), ((), ())), preferre...  77.4 us
  transfers between devices with their start and end apart: 19, of which 7 were waited for; matrix products, arithmetic and copies ran while one was open for 39% of the time, Pallas kernels for 0%

commit v1 on v0

v1 whole, which is shorter than its diff:
```python
import functools

import jax
import jax.numpy as jnp
from jax import lax
from jax.experimental import pallas as pl
from jax.experimental.pallas import tpu as pltpu
from jax.sharding import PartitionSpec as P

D = 768
HEADS = 12
HD = 64
FF = 3072
BLOCK = 64
LEN = 1024
NB = LEN // BLOCK
PAIRS = HEADS // 2
CHUNK = 256
PARTS = LEN // CHUNK
TILE = 256
EPS = 1e-06
MASKED = -1e30
BOTH = ("rep", "shard")
BF = jnp.bfloat16
F32 = jnp.float32
VMEM_LIMIT = 60 * 1024 * 1024


def nt(a, b):
    return lax.dot_general(a, b, (((1,), (1,)), ((), ())), preferred_element_type=F32)


def nn(a, b):
    return lax.dot_general(a, b, (((1,), (0,)), ((), ())), preferred_element_type=F32)


def tn(a, b):
    return lax.dot_general(a, b, (((0,), (0,)), ((), ())), preferred_element_type=F32)


def mask_rows(chosen):
    i = jnp.arange(NB, dtype=jnp.int32)[:, None]
    j = jnp.arange(NB, dtype=jnp.int32)[None, :]
    fixed = (i == 0) | (i == NB - 1) | (j == 0) | (j == NB - 1) | (jnp.abs(i - j) <= 1)
    picked = jnp.any(chosen[:, :, :, None] == j[None, None], axis=2)
    table = jnp.where(fixed[None] | picked, 0.0, MASKED).astype(F32)
    ends = jnp.full((HEADS, NB, 1), MASKED, F32)
    rest = jnp.zeros((HEADS, NB, 128 - NB - 1), F32)
    return jnp.concatenate([table, ends, rest], axis=2)


def key_columns(length):
    row = lax.broadcasted_iota(jnp.int32, (LEN, 128), 0)
    col = lax.broadcasted_iota(jnp.int32, (LEN, 128), 1)
    hot = ((col < NB) & (row // BLOCK == col)) | ((col == NB) & (row >= length))
    return hot.astype(BF)


def fill_operands(q_ref, k_ref, rows_ref, cols_ref, qa, ka):
    lane = lax.broadcasted_iota(jnp.int32, (1, 128), 1)
    q = q_ref[...].astype(F32) * (HD**-0.5)
    qa[0, :, :128] = jnp.where(lane < HD, q, 0.0).astype(BF)
    qa[1, :, :128] = jnp.where(lane >= HD, q, 0.0).astype(BF)
    for a in range(2):
        for i in range(NB):
            row = jnp.broadcast_to(rows_ref[a, i : i + 1, :], (BLOCK, 128))
            qa[a, i * BLOCK : (i + 1) * BLOCK, 128:] = row.astype(BF)
    ka[:, :128] = k_ref[...]
    ka[:, 128:] = cols_ref[...]


def attend_kernel(len_ref, q_ref, k_ref, v_ref, rows_ref, cols_ref, c_ref, lse_ref, qa, ka, stat):
    step = pl.program_id(0)
    length = len_ref[0]
    fill_operands(q_ref, k_ref, rows_ref, cols_ref, qa, ka)
    lane = lax.broadcasted_iota(jnp.int32, (CHUNK, 128), 1)
    parts = (length + CHUNK - 1) // CHUNK

    @pl.when(step == 0)
    def _():
        stat[...] = jnp.zeros_like(stat)

    def run(count):
        keys = count * CHUNK

        def body(c, carry):
            start = pl.multiple_of(c * CHUNK, CHUNK)
            here = pl.ds(start, CHUNK)
            outs = []
            held = stat[here, :]
            for a in range(2):
                s = nt(qa[a, here, :], ka[:keys, :])
                top = jnp.max(s, axis=1, keepdims=True)
                p = jnp.exp(s - top)
                total = jnp.sum(p, axis=1, keepdims=True)
                outs.append(nn(p.astype(BF), v_ref[:keys, :]) * (1.0 / total))
                held = jnp.where(lane == 2 * step + a, top + jnp.log(total), held)
            stat[here, :] = held
            row = start + lax.broadcasted_iota(jnp.int32, (CHUNK, 128), 0)
            out = jnp.where(lane < HD, outs[0], outs[1])
            c_ref[here, :] = jnp.where(row < length, out, 0.0).astype(BF)
            return carry

        lax.fori_loop(0, count, body, 0)
        if keys < LEN:
            c_ref[keys:, :] = jnp.zeros((LEN - keys, 128), BF)

    for count in range(1, PARTS + 1):
        pl.when(parts == count)(functools.partial(run, count))

    @pl.when(step == PAIRS - 1)
    def _():
        lse_ref[...] = stat[...].T[:16, :]


def attend(projected, rows, cols, length):
    pair = lambda base: pl.BlockSpec((LEN, 128), lambda h, n: (0, base + h))
    return pl.pallas_call(
        attend_kernel,
        name="attend",
        grid_spec=pltpu.PrefetchScalarGridSpec(
            num_scalar_prefetch=1,
            grid=(PAIRS,),
            in_specs=[
                pair(0),
                pair(PAIRS),
                pair(2 * PAIRS),
                pl.BlockSpec((2, NB, 128), lambda h, n: (h, 0, 0)),
                pl.BlockSpec((LEN, 128), lambda h, n: (0, 0)),
            ],
            out_specs=[pair(0), pl.BlockSpec((16, LEN), lambda h, n: (0, 0))],
            scratch_shapes=[
                pltpu.VMEM((2, LEN, 256), BF),
                pltpu.VMEM((LEN, 256), BF),
                pltpu.VMEM((LEN, 128), F32),
            ],
        ),
        out_shape=[jax.ShapeDtypeStruct((LEN, D), BF), jax.ShapeDtypeStruct((16, LEN), F32)],
        compiler_params=pltpu.CompilerParams(vmem_limit_bytes=VMEM_LIMIT),
        cost_estimate=pl.CostEstimate(flops=12 * 10**9, transcendentals=12 * 2**20, bytes_accessed=7 * 2**20),
    )(length, projected, projected, projected, rows, cols)


def attend_back_kernel(
    len_ref, q_ref, k_ref, v_ref, c_ref, g_ref, rows_ref, cols_ref, lse_ref, d_ref, sum_ref, qa, ka, ga, kt, delta, dq, dk, dv
):
    step = pl.program_id(0)
    length = len_ref[0]
    fill_operands(q_ref, k_ref, rows_ref, cols_ref, qa, ka)
    lane = lax.broadcasted_iota(jnp.int32, (1, 128), 1)
    g = g_ref[...].astype(F32)
    ga[0] = jnp.where(lane < HD, g, 0.0).astype(BF)
    ga[1] = jnp.where(lane >= HD, g, 0.0).astype(BF)
    prod = (g * c_ref[...].astype(F32)).T
    delta[0:1, :] = jnp.sum(prod[:HD], axis=0, keepdims=True)
    delta[1:2, :] = jnp.sum(prod[HD:], axis=0, keepdims=True)
    kt[...] = k_ref[...].astype(F32).T.astype(BF)
    dq[...] = jnp.zeros_like(dq)
    dk[...] = jnp.zeros_like(dk)
    dv[...] = jnp.zeros_like(dv)
    parts = (length + CHUNK - 1) // CHUNK

    def run(count):
        keys = count * CHUNK

        def body(c, carry):
            start = pl.multiple_of(c * CHUNK, CHUNK)
            here = pl.ds(start, CHUNK)
            for a in range(2):
                queries = qa[a, here, :]
                grads = ga[a, here, :]
                p = jnp.exp(nt(ka[:keys, :], queries) - lse_ref[pl.ds(2 * step + a, 1), here])
                ds = p * (nt(v_ref[:keys, :], grads) - delta[a : a + 1, here])
                p = p.astype(BF)
                ds = ds.astype(BF)
                dv[:keys, :] += nn(p, grads)
                dk[:keys, :] += nn(ds, queries[:, :128])
                dq[a * HD : (a + 1) * HD, here] = nn(kt[a * HD : (a + 1) * HD, :keys], ds)
            return carry

        lax.fori_loop(0, count, body, 0)

    for count in range(1, PARTS + 1):
        pl.when(parts == count)(functools.partial(run, count))

    grad_q = dq[...].T * (HD**-0.5)
    d_ref[0] = grad_q.astype(BF)
    d_ref[1] = dk[...].astype(BF)
    grad_v = dv[...]
    d_ref[2] = grad_v.astype(BF)
    sum_ref[0:1, :] = jnp.sum(grad_q, axis=0, keepdims=True)
    sum_ref[1:2, :] = jnp.sum(grad_v, axis=0, keepdims=True)
    sum_ref[2:8, :] = jnp.zeros((6, 128), F32)


def attend_back(projected, context, grads, rows, cols, lse, length):
    pair = lambda base: pl.BlockSpec((LEN, 128), lambda h, n: (0, base + h))
    return pl.pallas_call(
        attend_back_kernel,
        name="attend_back",
        grid_spec=pltpu.PrefetchScalarGridSpec(
            num_scalar_prefetch=1,
            grid=(PAIRS,),
            in_specs=[
                pair(0),
                pair(PAIRS),
                pair(2 * PAIRS),
                pair(0),
                pair(0),
                pl.BlockSpec((2, NB, 128), lambda h, n: (h, 0, 0)),
                pl.BlockSpec((LEN, 128), lambda h, n: (0, 0)),
                pl.BlockSpec((16, LEN), lambda h, n: (0, 0)),
            ],
            out_specs=[
                pl.BlockSpec((3, LEN, 128), lambda h, n: (0, 0, h)),
                pl.BlockSpec((8, 128), lambda h, n: (0, h)),
            ],
            scratch_shapes=[
                pltpu.VMEM((2, LEN, 256), BF),
                pltpu.VMEM((LEN, 256), BF),
                pltpu.VMEM((2, LEN, 128), BF),
                pltpu.VMEM((128, LEN), BF),
                pltpu.VMEM((8, LEN), F32),
                pltpu.VMEM((128, LEN), F32),
                pltpu.VMEM((LEN, 128), F32),
                pltpu.VMEM((LEN, 128), F32),
            ],
        ),
        out_shape=[jax.ShapeDtypeStruct((3, LEN, D), BF), jax.ShapeDtypeStruct((8, D), F32)],
        compiler_params=pltpu.CompilerParams(vmem_limit_bytes=VMEM_LIMIT),
        cost_estimate=pl.CostEstimate(flops=30 * 10**9, transcendentals=12 * 2**20, bytes_accessed=15 * 2**20),
    )(length, projected, projected, projected, context, grads, rows, cols, lse)


def gelu_parts(u):
    e = jnp.exp(-0.5 * u * u)
    t = 1.0 / (1.0 + (0.3275911 * 0.7071067811865476) * jnp.abs(u))
    poly = t * (0.127414796 + t * (-0.142248368 + t * (0.7107068705 + t * (-0.7265760135 + t * 0.5307027145))))
    tail = poly * e
    cdf = jnp.where(u >= 0, 1.0 - tail, tail)
    return u * cdf, cdf + u * (0.3989422804014327 * e)


def norm(hidden):
    center = hidden - jnp.mean(hidden, axis=-1, keepdims=True)
    inv = lax.rsqrt(jnp.mean(center * center, axis=-1, keepdims=True) + EPS)
    return center * inv, inv


def norm_back(grad, unit, inv, gain):
    e = gain * grad
    return inv * (e - jnp.mean(e, axis=-1, keepdims=True) - unit * jnp.mean(e * unit, axis=-1, keepdims=True))


def feed_kernel(
    len_ref, c_ref, x_ref, dy_ref, wo_ref, wu_ref, wd_ref, vec_ref, bu_ref,
    y_ref, n_ref, g_ref, dh2_ref, du_ref, dh1_ref, dc_ref, sums_ref, sumu_ref, slope
):
    step = pl.program_id(0)

    @pl.when(step == 0)
    def _():
        sums_ref[...] = jnp.zeros_like(sums_ref)
        sumu_ref[...] = jnp.zeros_like(sumu_ref)

    bias_out, gain1, shift1 = vec_ref[0:1, :], vec_ref[1:2, :], vec_ref[2:3, :]
    bias_down, gain2, shift2 = vec_ref[3:4, :], vec_ref[4:5, :], vec_ref[5:6, :]
    z1, r1 = norm(x_ref[...].astype(F32) + nn(c_ref[...], wo_ref[...]) + bias_out)
    n1 = z1 * gain1 + shift1
    low = n1.astype(BF)
    n_ref[...] = low
    total = n1 + bias_down
    for j in range(FF // D):
        cols = slice(j * D, (j + 1) * D)
        act, der = gelu_parts(nn(low, wu_ref[:, cols]) + bu_ref[:, cols])
        act = act.astype(BF)
        g_ref[:, cols] = act
        slope[:, cols] = der
        total = total + nn(act, wd_ref[cols, :])
    z2, r2 = norm(total)
    y_ref[...] = (z2 * gain2 + shift2).astype(BF)
    dy = dy_ref[...].astype(F32)
    dh2 = norm_back(dy, z2, r2, gain2)
    low = dh2.astype(BF)
    dh2_ref[...] = low
    sums_ref[5:6, :] += jnp.sum(dy * z2, axis=0, keepdims=True)
    sums_ref[6:7, :] += jnp.sum(dy, axis=0, keepdims=True)
    sums_ref[4:5, :] += jnp.sum(dh2, axis=0, keepdims=True)
    total = dh2
    for j in range(FF // D):
        cols = slice(j * D, (j + 1) * D)
        du = nt(low, wd_ref[cols, :]) * slope[:, cols]
        sumu_ref[0:1, cols] += jnp.sum(du, axis=0, keepdims=True)
        du = du.astype(BF)
        du_ref[:, cols] = du
        total = total + nt(du, wu_ref[:, cols])
    dh1 = norm_back(total, z1, r1, gain1)
    sums_ref[2:3, :] += jnp.sum(total * z1, axis=0, keepdims=True)
    sums_ref[3:4, :] += jnp.sum(total, axis=0, keepdims=True)
    sums_ref[1:2, :] += jnp.sum(dh1, axis=0, keepdims=True)
    low = dh1.astype(BF)
    dh1_ref[...] = low
    row = step * TILE + lax.broadcasted_iota(jnp.int32, (TILE, 1), 0)
    dc_ref[...] = jnp.where(row < len_ref[0], nt(low, wo_ref[...]), 0.0).astype(BF)


def feed(context, tokens, cotangent, w_out, w_up, w_down, vectors, bias_up, length):
    whole = lambda *shape: pl.BlockSpec(shape, lambda i, n: (0, 0), pipeline_mode=pl.Buffered(1))
    fixed = lambda *shape: pl.BlockSpec(shape, lambda i, n: (0, 0))
    tile = lambda width: pl.BlockSpec((TILE, width), lambda i, n: (i, 0))
    narrow = jax.ShapeDtypeStruct((LEN, D), BF)
    wide = jax.ShapeDtypeStruct((LEN, FF), BF)
    return pl.pallas_call(
        feed_kernel,
        name="feed",
        grid_spec=pltpu.PrefetchScalarGridSpec(
            num_scalar_prefetch=1,
            grid=(LEN // TILE,),
            in_specs=[
                tile(D), tile(D), tile(D), whole(D, D), whole(D, FF), whole(FF, D), fixed(8, D), fixed(1, FF)
            ],
            out_specs=[
                tile(D), tile(D), tile(FF), tile(D), tile(FF), tile(D), tile(D), fixed(8, D), fixed(8, FF)
            ],
            scratch_shapes=[pltpu.VMEM((TILE, FF), F32)],
        ),
        out_shape=[
            narrow, narrow, wide, narrow, wide, narrow, narrow,
            jax.ShapeDtypeStruct((8, D), F32), jax.ShapeDtypeStruct((8, FF), F32)
        ],
        compiler_params=pltpu.CompilerParams(vmem_limit_bytes=VMEM_LIMIT),
        cost_estimate=pl.CostEstimate(flops=22 * 10**9, transcendentals=3 * 2**20, bytes_accessed=36 * 2**20),
    )(length, context, tokens, cotangent, w_out, w_up, w_down, vectors, bias_up)


def tokens_back_kernel(d_ref, h_ref, w_ref, x_ref):
    total = h_ref[...].astype(F32)
    for j in range(3):
        total = total + nt(d_ref[j], w_ref[:, j * D : (j + 1) * D])
    x_ref[...] = total.astype(BF)


def tokens_back(grads, hidden, w_qkv):
    return pl.pallas_call(
        tokens_back_kernel,
        name="tokens_back",
        grid=(LEN // TILE,),
        in_specs=[
            pl.BlockSpec((3, TILE, D), lambda i: (0, i, 0)),
            pl.BlockSpec((TILE, D), lambda i: (i, 0)),
            pl.BlockSpec((D, 3 * D), lambda i: (0, 0), pipeline_mode=pl.Buffered(1)),
        ],
        out_specs=pl.BlockSpec((TILE, D), lambda i: (i, 0)),
        out_shape=jax.ShapeDtypeStruct((LEN, D), BF),
        compiler_params=pltpu.CompilerParams(vmem_limit_bytes=VMEM_LIMIT),
        cost_estimate=pl.CostEstimate(flops=4 * 10**9, transcendentals=0, bytes_accessed=12 * 2**20),
    )(grads, hidden, w_qkv)


def gather_rows(weight, rep, reps, shards):
    rows = weight.shape[0] // reps
    mine = lax.dynamic_slice_in_dim(weight, rep * rows, rows, 0)
    whole = lax.all_gather(mine, BOTH, axis=0, tiled=True)
    whole = whole.reshape(reps, shards, rows, weight.shape[1])
    return whole.transpose(1, 0, 2, 3).reshape(shards * reps * rows, weight.shape[1])


def reduce_rows(grad, reps, shards):
    rows = grad.shape[0] // (reps * shards)
    parts = grad.reshape(shards, reps, rows, grad.shape[1]).transpose(1, 0, 2, 3)
    parts = parts.reshape(grad.shape)
    mine = lax.psum_scatter(parts, BOTH, scatter_dimension=0, tiled=True)
    return lax.all_gather(mine, "rep", axis=0, tiled=True).astype(F32)


def per_device(
    inputs, cotangent, lengths, order, random_blocks,
    w_qkv, bias_query, bias_value, w_out, bias_out, gain_first, shift_first,
    w_up, bias_up, w_down, bias_down, gain_second, shift_second,
):
    device = lax.axis_index(BOTH)
    rep = lax.axis_index("rep")
    reps, shards = lax.axis_size("rep"), lax.axis_size("shard")
    seqs = reps * shards
    batches = inputs.shape[0]

    arrived = []
    for m in range(batches):
        sent = jnp.take(inputs[m], order[m], axis=0)
        got = lax.all_to_all(sent, BOTH, split_axis=0, concat_axis=0, tiled=True)
        arrived.append(got.reshape(LEN, D))
    packed = jnp.stack(
        [bias_query, bias_value, bias_out, gain_first, shift_first, bias_down, gain_second, shift_second]
        + list(bias_up.reshape(4, -1)), axis=0
    )
    vectors = lax.all_gather(packed[None], "shard", axis=0, tiled=True).astype(F32)
    small = vectors[:, :8].transpose(1, 0, 2).reshape(8, D)
    lift_bias = vectors[:, 8:].reshape(1, FF)
    feed_vectors = jnp.concatenate([small[2:], jnp.zeros((2, D), F32)], axis=0)
    bias_all = jnp.concatenate([small[0], jnp.zeros((D,), F32), small[1]])
    qkv = gather_rows(w_qkv, rep, reps, shards)
    out = gather_rows(w_out, rep, reps, shards)
    up = gather_rows(w_up, rep, reps, shards)
    down = gather_rows(w_down, rep, reps, shards)

    outputs, saved = [], []
    for m in range(batches):
        source = order[m, device]
        length = lengths[m, source]
        one = length.reshape(1)
        rows = mask_rows(random_blocks[m, source])
        cols = key_columns(length)
        tokens = arrived[m]
        projected = (jnp.dot(tokens, qkv, preferred_element_type=F32) + bias_all).astype(BF)
        context, lse = attend(projected, rows, cols, one)
        y, n1, g, dh2, du, dh1, dc, sums, sumu = feed(
            context, tokens, cotangent[m, 0], out, up, down, feed_vectors, lift_bias, one
        )
        back = lax.all_to_all(y.reshape(seqs, LEN // seqs, D), BOTH, split_axis=0, concat_axis=0, tiled=True)
        outputs.append(jnp.take(back, jnp.argsort(order[m]), axis=0))
        saved.append((projected, context, dc, rows, cols, lse, one, tokens, n1, g, dh2, du, dh1, sums, sumu))

    def both(left, right):
        return sum(tn(s[left], s[right]) for s in saved).astype(BF)

    grad_down = reduce_rows(both(9, 10), reps, shards)
    grad_up = reduce_rows(both(8, 11), reps, shards)
    grad_out = reduce_rows(both(1, 12), reps, shards)

    grad_inputs, grads, bias_sums = [], [], []
    for m in range(batches):
        projected, context, dc, rows, cols, lse, one = saved[m][:7]
        d3, dsum = attend_back(projected, context, dc, rows, cols, lse, one)
        dx = tokens_back(d3, saved[m][12], qkv)
        back = lax.all_to_all(dx.reshape(seqs, LEN // seqs, D), BOTH, split_axis=0, concat_axis=0, tiled=True)
        grad_inputs.append(jnp.take(back, jnp.argsort(order[m]), axis=0))
        grads.append(d3)
        bias_sums.append(dsum)
    grad_qkv = jnp.concatenate(
        [sum(tn(saved[m][7], grads[m][j]) for m in range(batches)).astype(BF) for j in range(3)], axis=1
    )
    grad_qkv = reduce_rows(grad_qkv, reps, shards)

    sums = sum(s[13] for s in saved)
    sumu = sum(s[14] for s in saved)[0].reshape(4, D)
    dsum = sum(bias_sums)
    rows12 = jnp.concatenate([dsum[0:2], sums[1:7], sumu], axis=0)
    rows12 = lax.psum(rows12, BOTH)
    shard = lax.axis_index("shard")
    width = D // shards
    own = lax.dynamic_slice_in_dim(rows12[:8], shard * width, width, 1)
    lift = lax.dynamic_slice_in_dim(rows12[8:].reshape(FF), shard * (FF // shards), FF // shards, 0)
    return (
        jnp.stack(outputs), jnp.stack(grad_inputs),
        grad_qkv, own[0], own[1], grad_out, own[2], own[3], own[4], grad_up, lift, grad_down, own[5], own[6], own[7],
    )


def solution(mesh):
    tokens = P(None, None, BOTH, None)
    placed = (
        tokens, P(None, BOTH, None, None), P(), P(), P(),
        P("shard", None), P("shard"), P("shard"), P("shard", None), P("shard"), P("shard"), P("shard"),
        P("shard", None), P("shard"), P("shard", None), P("shard"), P("shard"), P("shard"),
    )
    return jax.shard_map(
        per_device, mesh=mesh, in_specs=placed, out_specs=(tokens, tokens) + placed[5:], check_vma=False
    )
```

time: 2160 us -> 892 us (0.41)
  matrix products: 846 us -> 71.1 us
  local copies, waits for them, and re-layouts: 300 us -> 59.1 us
  waiting for transfers between devices: 559 us -> 345 us
  Pallas kernels: 0 us -> 170 us
  other arithmetic: 164 us -> 30.7 us
  blocking collectives: 222 us -> 114 us
  starting transfers between devices: 32.6 us -> 77.2 us
    dot_general x48 -> x14, matrix products: 846 us -> 71.1 us  [the longest x12 55.2 us: tn(): lax.dot_general(a, b, (((0,), (0,)), ((), ())), preferred_element_type=F32)]
    reduce_scatter x4, waiting for transfers between devices: 495 us -> 124 us  [reduce_rows(): mine = lax.psum_scatter(parts, BOTH, scatter_dimension=0, tiled=True)]
    pallas_call x0 -> x8, Pallas kernels: none -> 170 us  [the longest x2 85.9 us: feed(): pl.pallas_call(feed_kernel, name='feed', grid_spec=pltpu.PrefetchScalarGr...]
    while x2 -> x0, blocking collectives: 164 us -> none
    all_gather x8 -> x6, waiting for transfers between devices: 0.05 us -> 155 us  [the longest x4 120 us: gather_rows(): whole = lax.all_gather(mine, BOTH, axis=0, tiled=True)]
    reshape x4 -> x6, local copies, waits for them, and re-layouts: 133 us -> 15.1 us  [the longest x4 14.4 us: gather_rows(): whole = whole.reshape(reps, shards, rows, weight.shape[1])]
    reduce_sum x26 -> x0, other arithmetic: 64.7 us -> none  [the longest x4 45 us: attend_forward(): summed = jnp.sum(shifted, axis=-1, keepdims=True)]
    while x310 -> x0, local copies, waits for them, and re-layouts: 63.4 us -> none
  transfers between devices with their start and end apart: 19 -> 16, of which waited for: 7 -> 9; matrix products, arithmetic and copies ran while one was open for 39% -> 15% of each run, Pallas kernels for 0% -> 10%
where the time goes in v1:
time: 892 us; the launch traced here: 887 us
  waiting for transfers between devices  345 us (39%)
  Pallas kernels  170 us (19%)
  blocking collectives  114 us (13%)
  starting transfers between devices  77.2 us (9%)
  matrix products  71.1 us (8%)
  local copies, waits for them, and re-layouts  59.1 us (7%)
  other arithmetic  30.7 us (3%)
  between operations  19.3 us (2%)
    reduce_scatter x4, waiting for transfers between devices, reduce_rows(): mine = lax.psum_scatter(parts, BOTH, scatter_dimension=0, tiled=True)  124 us
    all_gather x4, waiting for transfers between devices, gather_rows(): whole = lax.all_gather(mine, BOTH, axis=0, tiled=True)  120 us
    pallas_call x2, Pallas kernels, feed(): pl.pallas_call(feed_kernel, name='feed', grid_spec=pltpu.PrefetchScalarGr...  85.9 us
    all_to_all x2, starting transfers between devices, per_device(): lax.all_to_all(dx.reshape(seqs, LEN // seqs, D), BOTH, split_axis=0, conc...  56.8 us
    dot_general x12, matrix products, tn(): lax.dot_general(a, b, (((0,), (0,)), ((), ())), preferred_element_type=F32)  55.2 us
    psum x1, blocking collectives, per_device(): rows12 = lax.psum(rows12, BOTH)  51.7 us
    all_gather x1, blocking collectives, per_device(): lax.all_gather(packed[None], 'shard', axis=0, tiled=True).astype(F32)  42.3 us
    pallas_call x2, Pallas kernels, attend_back(): pl.pallas_call(attend_back_kernel, name='attend_back', grid_spec=pltpu.Pr...  38.6 us
  transfers between devices with their start and end apart: 16, of which 9 were waited for; matrix products, arithmetic and copies ran while one was open for 15% of the time, Pallas kernels for 10%

profile of v1, /device:TPU:0, one launch (start us, length us, event | category | flops | bytes accessed | tf_op | source)
XLA Modules:
  0.0 887.2 jit_solution(9207260060453209712)
XLA Ops:
  31.3 42.3 %all-gather.1 = bf16[4,12,192]{2,1,0:T(8,128)(2,1)S(1)} all-gather(bf16[1,12,192]{2,1,0:T(8,128)(2,1)S(1)} %bitcast.157), channel_id=2, replica_groups=mesh['rep'=8,'shard'=4] {'shard'}, dimensions={0}, use_global_device_ids=true | all-gather | bytes 23040 | tf_op jit(solution)/shard_map/all_gather | solution.py:396
  98.6 41.6 %all-gather.9.cloned.1.call-done = bf16[768,2304]{1,0:T(8,128)(2,1)} async-done(((bf16[24,2304]{1,0:T(8,128)(2,1)}), bf16[768,2304]{1,0:T(8,128)(2,1)}) %all-gather.9.cloned.1.call-update) | async-done | bytes 3538960 | tf_op jit(solution)/shard_map/all_gather | solution.py:363
  142.4 8.5 add_convert_fusion.2.q_ref.k_ref.v_ref
  158.3 14.5 %attend.3 = (bf16[1024,768]{1,0:T(8,128)(2,1)}, f32[16,1024]{1,0:T(8,128)}) custom-call(s32[1]{0:T(128)} %bitcast.26.len_ref, bf16[1024,2304]{1,0:T(8,128)(2,1)} %add_convert_fusion.2.q_ref.k_ref.v_ref, bf16[1024,2304]{1,0:T(8,128)(2,1)} %add_convert_fusion.2.q_ref.k_ref.v_ref, bf16[1024,2304]{1,0:T(8,128)(2,1)} %add_convert_fusion.2.q_ref.k_ref.v_ref, ...), custom_call_target="tpu_custom_call" | custom-call | flops 12000000000 | bytes 7340032 | tf_op jit(solution)/shard_map/attend/pallas_call | solution.py:118
  172.9 14.7 %attend.2 = (bf16[1024,768]{1,0:T(8,128)(2,1)}, f32[16,1024]{1,0:T(8,128)}) custom-call(s32[1]{0:T(128)} %bitcast.2.len_ref, bf16[1024,2304]{1,0:T(8,128)(2,1)} %add_convert_fusion.3.q_ref.k_ref.v_ref, bf16[1024,2304]{1,0:T(8,128)(2,1)} %add_convert_fusion.3.q_ref.k_ref.v_ref, bf16[1024,2304]{1,0:T(8,128)(2,1)} %add_convert_fusion.3.q_ref.k_ref.v_ref, ...), custom_call_target="tpu_custom_call" | custom-call | flops 12000000000 | bytes 7340032 | tf_op jit(solution)/shard_map/attend/pallas_call | solution.py:118
  187.6 18.3 %all-gather.13.cloned.1.call-done = bf16[768,3072]{1,0:T(8,128)(2,1)} async-done(((bf16[24,3072]{1,0:T(8,128)(2,1)}), bf16[768,3072]{1,0:T(8,128)(2,1)}) %all-gather.13.cloned.1.call-update) | async-done | bytes 4718608 | tf_op jit(solution)/shard_map/all_gather | solution.py:363
  210.8 59.7 %all-gather.15.cloned.1.call-done = bf16[3072,768]{1,0:T(8,128)(2,1)} async-done(((bf16[96,768]{1,0:T(8,128)(2,1)}), bf16[3072,768]{1,0:T(8,128)(2,1)}) %all-gather.15.cloned.1.call-update) | async-done | bytes 4718608 | tf_op jit(solution)/shard_map/all_gather | solution.py:363
  275.4 42.8 %feed.2 = (bf16[1024,768]{1,0:T(8,128)(2,1)}, bf16[1024,768]{1,0:T(8,128)(2,1)}, bf16[1024,3072]{1,0:T(8,128)(2,1)}, bf16[1024,768]{1,0:T(8,128)(2,1)}, bf16[102...) custom-call(s32[1]{0:T(128)} %bitcast.2.len_ref, ...), custom_call_target="tpu_custom_call" | custom-call | flops 22000001024 | bytes 37748736 | tf_op jit(solution)/shard_map/feed/pallas_call | solution.py:313
  318.2 43.1 %feed.3 = (bf16[1024,768]{1,0:T(8,128)(2,1)}, bf16[1024,768]{1,0:T(8,128)(2,1)}, bf16[1024,3072]{1,0:T(8,128)(2,1)}, bf16[1024,768]{1,0:T(8,128)(2,1)}, bf16[102...) custom-call(s32[1]{0:T(128)} %bitcast.26.len_ref, ...), custom_call_target="tpu_custom_call" | custom-call | flops 22000001024 | bytes 37748736 | tf_op jit(solution)/shard_map/feed/pallas_call | solution.py:313
  377.7 8.0 fusion.37
  403.1 19.3 %attend_back.2 = (bf16[3,1024,768]{2,1,0:T(8,128)(2,1)}, f32[8,768]{1,0:T(8,128)}) custom-call(s32[1]{0:T(128)} %bitcast.2.len_ref, bf16[1024,2304]{1,0:T(8,128)(2,1)} %add_convert_fusion.3.q_ref.k_ref.v_ref, bf16[1024,2304]{1,0:T(8,128)(2,1)} %add_convert_fusion.3.q_ref.k_ref.v_ref, bf16[1024,2304]{1,0:T(8,128)(2,1)} %add_convert_fusion.3.q_ref.k_ref.v_ref, ...), custom_call_target="tpu_custom_call" | custom-call | flops 30000001024 | bytes 15728640 | tf_op jit(solution)/shard_map/attend_back/pallas_call | solution.py:198
  422.4 8.3 tokens_back.2
  430.7 19.3 %attend_back.3 = (bf16[3,1024,768]{2,1,0:T(8,128)(2,1)}, f32[8,768]{1,0:T(8,128)}) custom-call(s32[1]{0:T(128)} %bitcast.26.len_ref, bf16[1024,2304]{1,0:T(8,128)(2,1)} %add_convert_fusion.2.q_ref.k_ref.v_ref, bf16[1024,2304]{1,0:T(8,128)(2,1)} %add_convert_fusion.2.q_ref.k_ref.v_ref, bf16[1024,2304]{1,0:T(8,128)(2,1)} %add_convert_fusion.2.q_ref.k_ref.v_ref, ...), custom_call_target="tpu_custom_call" | custom-call | flops 30000001024 | bytes 15728640 | tf_op jit(solution)/shard_map/attend_back/pallas_call | solution.py:198
  463.7 52.4 %all-to-all-start.4 = ((bf16[32,32,768]{2,1,0:T(8,128)(2,1)}), bf16[32,32,768]{2,1,0:T(8,128)(2,1)}, u32[]{:S(2)}, u32[]{:S(2)}) async-start(bf16[32,32,768]{2,1,0:T(8,128)(2,1)} %bitcast.38), calls=%async_computation.4 | async-start | bytes 3145728 | tf_op jit(solution)/shard_map/all_to_all | solution.py:435
  535.4 29.1 %all-to-all-done.4 = bf16[32,32,768]{2,1,0:T(8,128)(2,1)} async-done(((bf16[32,32,768]{2,1,0:T(8,128)(2,1)}), bf16[32,32,768]{2,1,0:T(8,128)(2,1)}, u32[]{:S(2)}, u32[]{:S(2)}) %all-to-all-start.4) | async-done | bytes 1572896 | tf_op jit(solution)/shard_map/all_to_all | solution.py:435
  569.3 8.3 tokens_back.3
  577.6 36.2 %all-to-all-done.3 = bf16[32,32,768]{2,1,0:T(8,128)(2,1)S(1)} async-done(((bf16[32,32,768]{2,1,0:T(8,128)(2,1)}), bf16[32,32,768]{2,1,0:T(8,128)(2,1)S(1)}, u32[]{:S(2)}, u32[]{:S(2)}) %all-to-all-start.3) | async-done | bytes 1572896 | tf_op jit(solution)/shard_map/all_to_all | solution.py:419
  624.2 51.7 %psum.7 = f32[12,768]{1,0:T(8,128)S(1)} all-reduce(f32[12,768]{1,0:T(8,128)S(1)} %pad_maximum_fusion.3), channel_id=1, replica_groups=mesh['rep'=8,'shard'=4] {'rep','shard'}, use_global_device_ids=true, to_apply=%region_5.7 | all-reduce | flops 9216 | bytes 73728 | tf_op jit(solution)/shard_map/psum | solution.py:448
  677.3 41.5 %reduce-scatter.7.cloned.1.call-done = bf16[24,768]{1,0:T(8,128)(2,1)} async-done(((bf16[768,768]{1,0:T(8,128)(2,1)}), bf16[24,768]{1,0:T(8,128)(2,1)}) %reduce-scatter.7.cloned.1.call-update) | async-done | bytes 36880 | tf_op jit(solution)/shard_map/reduce_scatter | solution.py:372
  718.8 9.6 %all_gather.33 = bf16[192,768]{1,0:T(8,128)(2,1)S(1)} all-gather(bf16[24,768]{1,0:T(8,128)(2,1)} %reduce-scatter.7.cloned.1.call-done), channel_id=1, replica_groups=mesh['rep'=8,'shard'=4] {'rep'}, dimensions={0}, use_global_device_ids=true | all-gather | bytes 331776 | tf_op jit(solution)/shard_map/all_gather | solution.py:373
  744.4 82.3 %reduce-scatter.5.cloned.1.call-done = bf16[24,2304]{1,0:T(8,128)(2,1)} async-done(((bf16[768,2304]{1,0:T(8,128)(2,1)}), bf16[24,2304]{1,0:T(8,128)(2,1)}) %reduce-scatter.5.cloned.1.call-update) | async-done | bytes 110608 | tf_op jit(solution)/shard_map/reduce_scatter | solution.py:372
  826.7 10.7 %all_gather.32 = bf16[192,2304]{1,0:T(8,128)(2,1)S(1)} all-gather(bf16[24,2304]{1,0:T(8,128)(2,1)} %reduce-scatter.5.cloned.1.call-done), channel_id=1, replica_groups=mesh['rep'=8,'shard'=4] {'rep'}, dimensions={0}, use_global_device_ids=true | all-gather | bytes 995328 | tf_op jit(solution)/shard_map/all_gather | solution.py:373
  838.7 12.8 %all-gather.17.cloned.1.call-done = bf16[192,3072]{1,0:T(8,128)(2,1)} async-done(((bf16[24,3072]{1,0:T(8,128)(2,1)}), bf16[192,3072]{1,0:T(8,128)(2,1)}) %all-gather.17.cloned.1.call-update) | async-done | bytes 1179664 | tf_op jit(solution)/shard_map/all_gather | solution.py:373
  854.6 22.6 %all-gather.19.cloned.1.call-done = bf16[768,768]{1,0:T(8,128)(2,1)} async-done(((bf16[96,768]{1,0:T(8,128)(2,1)}), bf16[768,768]{1,0:T(8,128)(2,1)}) %all-gather.19.cloned.1.call-update) | async-done | bytes 1179664 | tf_op jit(solution)/shard_map/all_gather | solution.py:373
  (218 shorter events, 170.1 us)
Async XLA Ops:
  7.2 89.0 %all-gather.11.cloned.1.call-start = ((), (), s32[]{:S(2)}) async-start(), calls=%async_computation.11 | async-start | bytes 1216512 | tf_op jit(solution)/shard_map/all_gather | solution.py:363
  8.8 131.4 %all-gather.9.cloned.1.call-start = ((), (), s32[]{:S(2)}) async-start(), calls=%async_computation.10 | async-start | bytes 3649536 | tf_op jit(solution)/shard_map/all_gather | solution.py:363
  10.4 195.5 %all-gather.13.cloned.1.call-start = ((), (), s32[]{:S(2)}) async-start(), calls=%async_computation.12 | async-start | bytes 4866048 | tf_op jit(solution)/shard_map/all_gather | solution.py:363
  18.6 12.5 %copy-start.21 = (bf16[192]{0:T(256)(128)(2,1)S(1)}, bf16[192]{0:T(256)(128)(2,1)}, u32[]{:S(2)}) copy-start(bf16[192]{0:T(256)(128)(2,1)} %param.35) | copy-start | bytes 1156
  18.6 12.5 %copy-start.22 = (bf16[192]{0:T(256)(128)(2,1)S(1)}, bf16[192]{0:T(256)(128)(2,1)}, u32[]{:S(2)}) copy-start(bf16[192]{0:T(256)(128)(2,1)} %param.36) | copy-start | bytes 1156
  18.6 12.5 %copy-start.23 = (bf16[192]{0:T(256)(128)(2,1)S(1)}, bf16[192]{0:T(256)(128)(2,1)}, u32[]{:S(2)}) copy-start(bf16[192]{0:T(256)(128)(2,1)} %param.37) | copy-start | bytes 1156
  18.6 12.5 %copy-start.14 = (bf16[768]{0:T(1024)(128)(2,1)S(1)}, bf16[768]{0:T(1024)(128)(2,1)}, u32[]{:S(2)}) copy-start(bf16[768]{0:T(1024)(128)(2,1)} %param.33) | copy-start | bytes 4612
  18.7 60.3 %all-to-all-start.2 = ((bf16[32,32,768]{2,1,0:T(8,128)(2,1)}), bf16[32,32,768]{2,1,0:T(8,128)(2,1)}, u32[]{:S(2)}, u32[]{:S(2)}) async-start(bf16[32,32,768]{2,1,0:T(8,128)(2,1)} %broadcast_select_fusion), calls=%async_computation.2 | async-start | bytes 3145728 | tf_op jit(solution)/shard_map/all_to_all | solution.py:390
  26.1 244.4 %all-gather.15.cloned.1.call-start = ((), (), s32[]{:S(2)}) async-start(), calls=%async_computation.13 | async-start | bytes 4866048 | tf_op jit(solution)/shard_map/all_gather | solution.py:363
  79.0 15.3 %copy-start.7 = (bf16[2,1,1024,768]{3,2,1,0:T(8,128)(2,1)S(1)}, bf16[2,1,1024,768]{3,2,1,0:T(8,128)(2,1)}, u32[]{:S(2)}) copy-start(bf16[2,1,1024,768]{3,2,1,0:T(8,128)(2,1)} %param.21) | copy-start | bytes 9437188
  79.0 72.0 %all-to-all-start = ((bf16[32,32,768]{2,1,0:T(8,128)(2,1)}), bf16[32,32,768]{2,1,0:T(8,128)(2,1)}, u32[]{:S(2)}, u32[]{:S(2)}) async-start(bf16[32,32,768]{2,1,0:T(8,128)(2,1)} %broadcast_select_fusion.1), calls=%async_computation | async-start | bytes 3145728 | tf_op jit(solution)/shard_map/all_to_all | solution.py:390
  83.9 534.4 %reduce-scatter.9.cloned.1.call-start = ((), (), s32[]{:S(2)}) async-start(), calls=%async_computation.16 | async-start | bytes 4866048 | tf_op jit(solution)/shard_map/reduce_scatter | solution.py:372
  318.2 43.1 %copy-start.24 = (bf16[1024,768]{1,0:T(8,128)(2,1)S(1)}, bf16[1024,768]{1,0:T(8,128)(2,1)}, u32[]{:S(2)}) copy-start(bf16[1024,768]{1,0:T(8,128)(2,1)} %get-tuple-element.64) | copy-start | bytes 4718596
  377.6 245.8 %reduce-scatter.11.cloned.1.call-start = ((), (), s32[]{:S(2)}) async-start(), calls=%async_computation.18 | async-start | bytes 4866048 | tf_op jit(solution)/shard_map/reduce_scatter | solution.py:372
  394.2 68.3 %all-to-all-start.1 = ((bf16[32,32,768]{2,1,0:T(8,128)(2,1)}), bf16[32,32,768]{2,1,0:T(8,128)(2,1)S(1)}, u32[]{:S(2)}, u32[]{:S(2)}) async-start(bf16[32,32,768]{2,1,0:T(8,128)(2,1)} %bitcast.22), calls=%async_computation.1 | async-start | bytes 3145728 | tf_op jit(solution)/shard_map/all_to_all | solution.py:419
  397.2 321.6 %reduce-scatter.7.cloned.1.call-start = ((), (), s32[]{:S(2)}) async-start(), calls=%async_computation.15 | async-start | bytes 1216512 | tf_op jit(solution)/shard_map/reduce_scatter | solution.py:372
  463.7 100.8 %all-to-all-start.4 = ((bf16[32,32,768]{2,1,0:T(8,128)(2,1)}), bf16[32,32,768]{2,1,0:T(8,128)(2,1)}, u32[]{:S(2)}, u32[]{:S(2)}) async-start(bf16[32,32,768]{2,1,0:T(8,128)(2,1)} %bitcast.38), calls=%async_computation.4 | async-start | bytes 3145728 | tf_op jit(solution)/shard_map/all_to_all | solution.py:435
  516.1 310.6 %reduce-scatter.5.cloned.1.call-start = ((), (), s32[]{:S(2)}) async-start(), calls=%async_computation.14 | async-start | bytes 3649536 | tf_op jit(solution)/shard_map/reduce_scatter | solution.py:372
  564.5 49.3 %all-to-all-start.3 = ((bf16[32,32,768]{2,1,0:T(8,128)(2,1)}), bf16[32,32,768]{2,1,0:T(8,128)(2,1)S(1)}, u32[]{:S(2)}, u32[]{:S(2)}) async-start(bf16[32,32,768]{2,1,0:T(8,128)(2,1)} %bitcast.36), calls=%async_computation.3 | async-start | bytes 3145728 | tf_op jit(solution)/shard_map/all_to_all | solution.py:419
  613.8 121.1 %all-to-all-start.5 = ((bf16[32,32,768]{2,1,0:T(8,128)(2,1)}), bf16[32,32,768]{2,1,0:T(8,128)(2,1)}, u32[]{:S(2)}, u32[]{:S(2)}) async-start(bf16[32,32,768]{2,1,0:T(8,128)(2,1)} %bitcast.150), calls=%async_computation.5 | async-start | bytes 3145728 | tf_op jit(solution)/shard_map/all_to_all | solution.py:435
  618.3 110.9 %copy-start.3 = (bf16[32,32,768]{2,1,0:T(8,128)(2,1)S(1)}, bf16[32,32,768]{2,1,0:T(8,128)(2,1)}, u32[]{:S(2)}) copy-start(bf16[32,32,768]{2,1,0:T(8,128)(2,1)} %copy-done.2) | copy-start | bytes 4718596
  618.3 233.3 %all-gather.17.cloned.1.call-start = ((), (), s32[]{:S(2)}) async-start(), calls=%async_computation.17 | async-start | bytes 1327104 | tf_op jit(solution)/shard_map/all_gather | solution.py:373
  619.0 258.2 %all-gather.19.cloned.1.call-start = ((), (), s32[]{:S(2)}) async-start(), calls=%async_computation.19 | async-start | bytes 1327104 | tf_op jit(solution)/shard_map/all_gather | solution.py:373
  851.5 28.5 %copy-start.1 = (bf16[192,3072]{1,0:T(8,128)(2,1)S(1)}, bf16[192,3072]{1,0:T(8,128)(2,1)}, u32[]{:S(2)}) copy-start(bf16[192,3072]{1,0:T(8,128)(2,1)} %param.32) | copy-start | bytes 3538948
  (26 other events, 187.8 us)
Sparse Core Ops, SparseCore 0:
  10.8 61.1 all-gather.10
  74.8 65.3 all-gather.8
  143.6 62.3 all-gather.12
  208.6 61.9 all-gather.14
  377.7 109.0 reduce-scatter.8
  492.2 125.6 reduce-scatter.10
  622.9 95.7 reduce-scatter.6
  724.2 102.4 reduce-scatter.4
  828.6 22.8 all-gather.16
  853.3 23.9 all-gather.18

commit v2 on v1

--- a/solution.py
+++ b/solution.py
@@ -357,20 +357,22 @@
     )(grads, hidden, w_qkv)
 
 
-def gather_rows(weight, rep, reps, shards):
-    rows = weight.shape[0] // reps
-    mine = lax.dynamic_slice_in_dim(weight, rep * rows, rows, 0)
-    whole = lax.all_gather(mine, BOTH, axis=0, tiled=True)
-    whole = whole.reshape(reps, shards, rows, weight.shape[1])
-    return whole.transpose(1, 0, 2, 3).reshape(shards * reps * rows, weight.shape[1])
-
-
-def reduce_rows(grad, reps, shards):
-    rows = grad.shape[0] // (reps * shards)
-    parts = grad.reshape(shards, reps, rows, grad.shape[1]).transpose(1, 0, 2, 3)
-    parts = parts.reshape(grad.shape)
-    mine = lax.psum_scatter(parts, BOTH, scatter_dimension=0, tiled=True)
-    return lax.all_gather(mine, "rep", axis=0, tiled=True).astype(F32)
+def up8(rows):
+    return -(-rows // 8) * 8
+
+
+def wide_rows(block):
+    return jnp.concatenate([block[..., j * D : (j + 1) * D] for j in range(block.shape[-1] // D)], axis=-2)
+
+
+def rows_wide(block, count):
+    reps, shards, rows = block.shape[0], block.shape[1], block.shape[2] // count
+    block = block.reshape(reps, shards, count, rows, D).transpose(1, 0, 3, 2, 4)
+    return block.reshape(shards * reps * rows, count * D)
+
+
+def parts_of(grad, reps, shards):
+    return grad.reshape(shards, reps, -1, D).transpose(1, 0, 2, 3)
 
 
 def per_device(
@@ -389,67 +391,84 @@
         sent = jnp.take(inputs[m], order[m], axis=0)
         got = lax.all_to_all(sent, BOTH, split_axis=0, concat_axis=0, tiled=True)
         arrived.append(got.reshape(LEN, D))
+    part = lambda weight: lax.dynamic_slice_in_dim(weight, rep * (weight.shape[0] // reps), weight.shape[0] // reps, 0)
+    rows = D // seqs
     packed = jnp.stack(
         [bias_query, bias_value, bias_out, gain_first, shift_first, bias_down, gain_second, shift_second]
-        + list(bias_up.reshape(4, -1)), axis=0
-    )
-    vectors = lax.all_gather(packed[None], "shard", axis=0, tiled=True).astype(F32)
+        + list(bias_up.reshape(FF // D, -1)), axis=0
+    ).reshape(-1, D)
+    extra = packed.shape[0]
+    pad = jnp.zeros((up8(3 * rows + extra) - 3 * rows - extra, D), BF)
+    first = jnp.concatenate([wide_rows(part(w_qkv)), packed, pad], axis=0)
+    first = lax.all_gather(first, BOTH, axis=0).reshape(reps, shards, -1, D)
+    qkv = rows_wide(first[:, :, : 3 * rows], 3)
+    vectors = first[0, :, 3 * rows : 3 * rows + extra].astype(F32).reshape(shards, -1, D // shards)
     small = vectors[:, :8].transpose(1, 0, 2).reshape(8, D)
     lift_bias = vectors[:, 8:].reshape(1, FF)
     feed_vectors = jnp.concatenate([small[2:], jnp.zeros((2, D), F32)], axis=0)
     bias_all = jnp.concatenate([small[0], jnp.zeros((D,), F32), small[1]])
-    qkv = gather_rows(w_qkv, rep, reps, shards)
-    out = gather_rows(w_out, rep, reps, shards)
-    up = gather_rows(w_up, rep, reps, shards)
-    down = gather_rows(w_down, rep, reps, shards)
+    rest = jnp.concatenate([part(w_out), wide_rows(part(w_up)), part(w_down)], axis=0)
+    rest = lax.all_gather(rest, BOTH, axis=0).reshape(reps, shards, -1, D)
+    out = rows_wide(rest[:, :, :rows], 1)
+    up = rows_wide(rest[:, :, rows : 5 * rows], 4)
+    down = rows_wide(rest[:, :, 5 * rows :], 1)
 
     outputs, saved = [], []
     for m in range(batches):
         source = order[m, device]
         length = lengths[m, source]
         one = length.reshape(1)
-        rows = mask_rows(random_blocks[m, source])
+        table = mask_rows(random_blocks[m, source])
         cols = key_columns(length)
         tokens = arrived[m]
         projected = (jnp.dot(tokens, qkv, preferred_element_type=F32) + bias_all).astype(BF)
-        context, lse = attend(projected, rows, cols, one)
+        context, lse = attend(projected, table, cols, one)
         y, n1, g, dh2, du, dh1, dc, sums, sumu = feed(
             context, tokens, cotangent[m, 0], out, up, down, feed_vectors, lift_bias, one
         )
         back = lax.all_to_all(y.reshape(seqs, LEN // seqs, D), BOTH, split_axis=0, concat_axis=0, tiled=True)
         outputs.append(jnp.take(back, jnp.argsort(order[m]), axis=0))
-        saved.append((projected, context, dc, rows, cols, lse, one, tokens, n1, g, dh2, du, dh1, sums, sumu))
+        saved.append((projected, context, dc, table, cols, lse, one, tokens, n1, g, dh2, du, dh1, sums, sumu))
 
     def both(left, right):
         return sum(tn(s[left], s[right]) for s in saved).astype(BF)
 
-    grad_down = reduce_rows(both(9, 10), reps, shards)
-    grad_up = reduce_rows(both(8, 11), reps, shards)
-    grad_out = reduce_rows(both(1, 12), reps, shards)
+    grad_up = both(8, 11).reshape(shards, reps, rows, FF).transpose(1, 0, 2, 3)
+    parts = jnp.concatenate(
+        [parts_of(both(1, 12), reps, shards), wide_rows(grad_up), parts_of(both(9, 10), reps, shards)], axis=2
+    )
+    mine = lax.psum_scatter(parts.reshape(-1, D), BOTH, scatter_dimension=0, tiled=True)
+    mine = lax.all_gather(mine, "rep", axis=0)
+    grad_out = rows_wide(mine[:, None, :rows], 1).astype(F32)
+    grad_up = rows_wide(mine[:, None, rows : 5 * rows], 4).astype(F32)
+    grad_down = rows_wide(mine[:, None, 5 * rows :], 1).astype(F32)
 
     grad_inputs, grads, bias_sums = [], [], []
     for m in range(batches):
-        projected, context, dc, rows, cols, lse, one = saved[m][:7]
-        d3, dsum = attend_back(projected, context, dc, rows, cols, lse, one)
+        projected, context, dc, table, cols, lse, one = saved[m][:7]
+        d3, dsum = attend_back(projected, context, dc, table, cols, lse, one)
         dx = tokens_back(d3, saved[m][12], qkv)
         back = lax.all_to_all(dx.reshape(seqs, LEN // seqs, D), BOTH, split_axis=0, concat_axis=0, tiled=True)
         grad_inputs.append(jnp.take(back, jnp.argsort(order[m]), axis=0))
         grads.append(d3)
         bias_sums.append(dsum)
-    grad_qkv = jnp.concatenate(
-        [sum(tn(saved[m][7], grads[m][j]) for m in range(batches)).astype(BF) for j in range(3)], axis=1
-    )
-    grad_qkv = reduce_rows(grad_qkv, reps, shards)
-
     sums = sum(s[13] for s in saved)
-    sumu = sum(s[14] for s in saved)[0].reshape(4, D)
+    sumu = sum(s[14] for s in saved)[0].reshape(FF // D, D)
     dsum = sum(bias_sums)
-    rows12 = jnp.concatenate([dsum[0:2], sums[1:7], sumu], axis=0)
-    rows12 = lax.psum(rows12, BOTH)
-    shard = lax.axis_index("shard")
-    width = D // shards
-    own = lax.dynamic_slice_in_dim(rows12[:8], shard * width, width, 1)
-    lift = lax.dynamic_slice_in_dim(rows12[8:].reshape(FF), shard * (FF // shards), FF // shards, 0)
+    sums = jnp.concatenate([dsum[0:2], sums[1:7]], axis=0).reshape(8, shards, -1).transpose(1, 0, 2)
+    sums = jnp.concatenate([sums, sumu.reshape(shards, FF // D, -1)], axis=1).astype(BF).reshape(1, shards, extra, D)
+    sums = jnp.broadcast_to(sums, (reps, shards, extra, D))
+    blank = jnp.zeros((reps, shards) + pad.shape, BF)
+    parts = [
+        parts_of(sum(tn(saved[m][7], grads[m][j]) for m in range(batches)).astype(BF), reps, shards) for j in range(3)
+    ]
+    parts = jnp.concatenate(parts + [sums, blank], axis=2).reshape(seqs, -1, D)
+    parts = lax.all_to_all(parts, BOTH, split_axis=0, concat_axis=0, tiled=True)
+    mine = jnp.sum(parts.astype(F32), axis=0).astype(BF)
+    mine = lax.all_gather(mine, "rep", axis=0)
+    grad_qkv = rows_wide(mine[:, None, : 3 * rows], 3).astype(F32)
+    own = mine[0, 3 * rows : 3 * rows + extra].astype(F32).reshape(-1, D // shards)
+    lift = own[8:].reshape(FF // shards)
     return (
         jnp.stack(outputs), jnp.stack(grad_inputs),
         grad_qkv, own[0], own[1], grad_out, own[2], own[3], own[4], grad_up, lift, grad_down, own[5], own[6], own[7],

time: 892 us -> 737 us (0.83)
  waiting for transfers between devices: 345 us -> 207 us
  blocking collectives: 114 us -> 12.3 us
  local copies, waits for them, and re-layouts: 59.1 us -> 109 us
  starting transfers between devices: 77.2 us -> 101 us
  Pallas kernels: 170 us -> 179 us
    all_gather x6 -> x3, waiting for transfers between devices: 155 us -> 4.73 us  [the longest x1 4.73 us: per_device(): rest = lax.all_gather(rest, BOTH, axis=0).reshape(reps, shards, -1, D)]
    reduce_scatter x4 -> x1, waiting for transfers between devices: 124 us -> 0.02 us  [per_device(): lax.psum_scatter(parts.reshape(-1, D), BOTH, scatter_dimension=0, tiled=T...]
    all_to_all x0 -> x1, waiting for transfers between devices: none -> 66.9 us  [per_device(): parts = lax.all_to_all(parts, BOTH, split_axis=0, concat_axis=0, tiled=True)]
    all_to_all x2, waiting for transfers between devices: 0.01 us -> 63.4 us  [per_device(): got = lax.all_to_all(sent, BOTH, split_axis=0, concat_axis=0, tiled=True)]
    psum x1 -> x0, blocking collectives: 51.7 us -> none  [per_device(): rows12 = lax.psum(rows12, BOTH)]
    all_gather x3 -> x1, blocking collectives: 62.6 us -> 12.3 us  [per_device(): mine = lax.all_gather(mine, 'rep', axis=0)]
    all_to_all x2, starting transfers between devices: 7.68 us -> 38.1 us  [per_device(): lax.all_to_all(y.reshape(seqs, LEN // seqs, D), BOTH, split_axis=0, conca...]
    all_to_all x2, waiting for transfers between devices: 29.1 us -> 59 us  [per_device(): lax.all_to_all(dx.reshape(seqs, LEN // seqs, D), BOTH, split_axis=0, conc...]
  transfers between devices with their start and end apart: 16 -> 11, of which waited for: 9 -> 6; matrix products, arithmetic and copies ran while one was open for 15% -> 23% of each run, Pallas kernels for 10% -> 19%
where the time goes in v2:
time: 737 us; the launch traced here: 724 us
  waiting for transfers between devices  207 us (28%)
  Pallas kernels  179 us (24%)
  local copies, waits for them, and re-layouts  109 us (15%)
  starting transfers between devices  101 us (14%)
  matrix products  69.9 us (9%)
  other arithmetic  27.3 us (4%)
  between operations  18.9 us (3%)
  blocking collectives  12.3 us (2%)
    pallas_call x2, Pallas kernels, feed(): pl.pallas_call(feed_kernel, name='feed', grid_spec=pltpu.PrefetchScalarGr...  86 us
    all_to_all x1, waiting for transfers between devices, per_device(): parts = lax.all_to_all(parts, BOTH, split_axis=0, concat_axis=0, tiled=True)  66.9 us
    all_to_all x2, waiting for transfers between devices, per_device(): got = lax.all_to_all(sent, BOTH, split_axis=0, concat_axis=0, tiled=True)  63.4 us
    all_to_all x2, waiting for transfers between devices, per_device(): lax.all_to_all(dx.reshape(seqs, LEN // seqs, D), BOTH, split_axis=0, conc...  59 us
    dot_general x12, matrix products, tn(): lax.dot_general(a, b, (((0,), (0,)), ((), ())), preferred_element_type=F32)  54.6 us
    all_to_all x2, starting transfers between devices, per_device(): lax.all_to_all(dx.reshape(seqs, LEN // seqs, D), BOTH, split_axis=0, conc...  44.1 us
    pallas_call x2, Pallas kernels, attend_back(): pl.pallas_call(attend_back_kernel, name='attend_back', grid_spec=pltpu.Pr...  42.5 us
    all_to_all x2, starting transfers between devices, per_device(): lax.all_to_all(y.reshape(seqs, LEN // seqs, D), BOTH, split_axis=0, conca...  38.1 us
  transfers between devices with their start and end apart: 11, of which 6 were waited for; matrix products, arithmetic and copies ran while one was open for 23% of the time, Pallas kernels for 19%

profile of v2, /device:TPU:0, one launch (start us, length us, event | category | flops | bytes accessed | tf_op | source)
XLA Modules:
  0.0 724.3 jit_solution(15572062558029711457)
XLA Ops:
  29.2 7.4 %all-to-all-start.2 = ((bf16[32,32,768]{2,1,0:T(8,128)(2,1)}), bf16[32,32,768]{2,1,0:T(8,128)(2,1)}, u32[]{:S(2)}, u32[]{:S(2)}) async-start(bf16[32,32,768]{2,1,0:T(8,128)(2,1)} %broadcast_select_fusion), calls=%async_computation.2 | async-start | bytes 3145728 | tf_op jit(solution)/shard_map/all_to_all | solution.py:392
  47.1 41.5 %all-to-all-done.2 = bf16[32,32,768]{2,1,0:T(8,128)(2,1)} async-done(((bf16[32,32,768]{2,1,0:T(8,128)(2,1)}), bf16[32,32,768]{2,1,0:T(8,128)(2,1)}, u32[]{:S(2)}, u32[]{:S(2)}) %all-to-all-start.2) | async-done | bytes 1572896 | tf_op jit(solution)/shard_map/all_to_all | solution.py:392
  116.7 8.0 %add_convert_fusion.2.q_ref.k_ref.v_ref = bf16[1024,2304]{1,0:T(8,128)(2,1)} fusion(bf16[1024,768]{1,0:T(8,128)(2,1)} %bitcast.27.x_ref, bf16[768,2304]{1,0:T(8,128)(2,1)S(1)} %bitcast.197, f32[2304]{0:T(1024)S(1)} %pad_maximum_fusion.3), kind=kOutput, calls=%fused_computation.8 | convolution fusion | flops 3628597248 | bytes 9839616 | tf_op jit(solution)/shard_map/dot_general | solution.py:424
  124.7 21.9 %all-to-all-done = bf16[32,32,768]{2,1,0:T(8,128)(2,1)} async-done(((bf16[32,32,768]{2,1,0:T(8,128)(2,1)}), bf16[32,32,768]{2,1,0:T(8,128)(2,1)}, u32[]{:S(2)}, u32[]{:S(2)}) %all-to-all-start) | async-done | bytes 1572896 | tf_op jit(solution)/shard_map/all_to_all | solution.py:392
  146.5 7.3 %add_convert_fusion.3.q_ref.k_ref.v_ref = bf16[1024,2304]{1,0:T(8,128)(2,1)} fusion(bf16[1024,768]{1,0:T(8,128)(2,1)} %bitcast.4.x_ref, bf16[768,2304]{1,0:T(8,128)(2,1)S(1)} %bitcast.198, f32[2304]{0:T(1024)} %copy-done.10), kind=kOutput, calls=%fused_computation.9 | convolution fusion | flops 3628597248 | bytes 9839616 | tf_op jit(solution)/shard_map/dot_general | solution.py:424
  153.8 23.8 %attend.3 = (bf16[1024,768]{1,0:T(8,128)(2,1)}, f32[16,1024]{1,0:T(8,128)}) custom-call(s32[1]{0:T(128)} %bitcast.25.len_ref, bf16[1024,2304]{1,0:T(8,128)(2,1)} %add_convert_fusion.2.q_ref.k_ref.v_ref, bf16[1024,2304]{1,0:T(8,128)(2,1)} %add_convert_fusion.2.q_ref.k_ref.v_ref, bf16[1024,2304]{1,0:T(8,128)(2,1)} %add_convert_fusion.2.q_ref.k_ref.v_ref, ...), custom_call_target="tpu_custom_call" | custom-call | flops 12000000000 | bytes 7340032 | tf_op jit(solution)/shard_map/attend/pallas_call | solution.py:118
  177.6 10.3 %attend.2 = (bf16[1024,768]{1,0:T(8,128)(2,1)}, f32[16,1024]{1,0:T(8,128)}) custom-call(s32[1]{0:T(128)} %bitcast.2.len_ref, bf16[1024,2304]{1,0:T(8,128)(2,1)} %add_convert_fusion.3.q_ref.k_ref.v_ref, bf16[1024,2304]{1,0:T(8,128)(2,1)} %add_convert_fusion.3.q_ref.k_ref.v_ref, bf16[1024,2304]{1,0:T(8,128)(2,1)} %add_convert_fusion.3.q_ref.k_ref.v_ref, ...), custom_call_target="tpu_custom_call" | custom-call | flops 12000000000 | bytes 7340032 | tf_op jit(solution)/shard_map/attend/pallas_call | solution.py:118
  208.9 42.9 %feed.2 = (bf16[1024,768]{1,0:T(8,128)(2,1)}, bf16[1024,768]{1,0:T(8,128)(2,1)}, bf16[1024,3072]{1,0:T(8,128)(2,1)}, bf16[1024,768]{1,0:T(8,128)(2,1)}, bf16[102...) custom-call(s32[1]{0:T(128)} %bitcast.2.len_ref, ...), custom_call_target="tpu_custom_call" | custom-call | flops 22000001024 | bytes 37748736 | tf_op jit(solution)/shard_map/feed/pallas_call | solution.py:313
  251.8 34.1 %all-to-all-start.1 = ((bf16[32,32,768]{2,1,0:T(8,128)(2,1)}), bf16[32,32,768]{2,1,0:T(8,128)(2,1)S(1)}, u32[]{:S(2)}, u32[]{:S(2)}) async-start(bf16[32,32,768]{2,1,0:T(8,128)(2,1)} %bitcast.209), calls=%async_computation.1 | async-start | bytes 3145728 | tf_op jit(solution)/shard_map/all_to_all | solution.py:429
  290.2 43.1 %feed.3 = (bf16[1024,768]{1,0:T(8,128)(2,1)}, bf16[1024,768]{1,0:T(8,128)(2,1)}, bf16[1024,3072]{1,0:T(8,128)(2,1)}, bf16[1024,768]{1,0:T(8,128)(2,1)}, bf16[102...) custom-call(s32[1]{0:T(128)} %bitcast.25.len_ref, ...), custom_call_target="tpu_custom_call" | custom-call | flops 22000001024 | bytes 37748736 | tf_op jit(solution)/shard_map/feed/pallas_call | solution.py:313
  338.8 8.0 %fusion.42 = f32[768,3072]{1,0:T(8,128)S(1)} fusion(bf16[1024,768]{1,0:T(8,128)(2,1)S(1)} %copy-done.14, bf16[1024,3072]{1,0:T(8,128)(2,1)} %get-tuple-element.65), kind=kOutput, calls=%fused_computation.137 | convolution fusion | flops 4831838208 | bytes 17301504 | tf_op jit(solution)/shard_map/dot_general | solution.py:38
  357.7 7.9 %fusion.43 = f32[3072,768]{1,0:T(8,128)S(1)} fusion(bf16[1024,3072]{1,0:T(8,128)(2,1)} %get-tuple-element.68, bf16[1024,768]{1,0:T(8,128)(2,1)S(1)} %copy-done.18), kind=kOutput, calls=%fused_computation.138 | convolution fusion | flops 4831838208 | bytes 17301504 | tf_op jit(solution)/shard_map/dot_general | solution.py:38
  374.2 13.1 %attend_back.2 = (bf16[3,1024,768]{2,1,0:T(8,128)(2,1)}, f32[8,768]{1,0:T(8,128)}) custom-call(s32[1]{0:T(128)} %bitcast.2.len_ref, bf16[1024,2304]{1,0:T(8,128)(2,1)} %add_convert_fusion.3.q_ref.k_ref.v_ref, bf16[1024,2304]{1,0:T(8,128)(2,1)} %add_convert_fusion.3.q_ref.k_ref.v_ref, bf16[1024,2304]{1,0:T(8,128)(2,1)} %add_convert_fusion.3.q_ref.k_ref.v_ref, ...), custom_call_target="tpu_custom_call" | custom-call | flops 30000001024 | bytes 15728640 | tf_op jit(solution)/shard_map/attend_back/pallas_call | solution.py:198
  387.4 8.6 %tokens_back.2 = bf16[1024,768]{1,0:T(8,128)(2,1)} custom-call(bf16[3,1024,768]{2,1,0:T(8,128)(2,1)} %get-tuple-element.52.d_ref, bf16[1024,768]{1,0:T(8,128)(2,1)} %get-tuple-element.53.h_ref, bf16[768,2304]{1,0:T(8,128)(2,1)} %bitcast.199), custom_call_target="tpu_custom_call" | custom-call | flops 4000000000 | bytes 12582912 | tf_op jit(solution)/shard_map/tokens_back/pallas_call | solution.py:344
  396.0 36.0 %all-to-all-start.4 = ((bf16[32,32,768]{2,1,0:T(8,128)(2,1)}), bf16[32,32,768]{2,1,0:T(8,128)(2,1)S(1)}, u32[]{:S(2)}, u32[]{:S(2)}) async-start(bf16[32,32,768]{2,1,0:T(8,128)(2,1)} %bitcast.211), calls=%async_computation.4 | async-start | bytes 3145728 | tf_op jit(solution)/shard_map/all_to_all | solution.py:451
  433.1 59.0 %all-to-all-done.4 = bf16[32,32,768]{2,1,0:T(8,128)(2,1)S(1)} async-done(((bf16[32,32,768]{2,1,0:T(8,128)(2,1)}), bf16[32,32,768]{2,1,0:T(8,128)(2,1)S(1)}, u32[]{:S(2)}, u32[]{:S(2)}) %all-to-all-start.4) | async-done | bytes 1572896 | tf_op jit(solution)/shard_map/all_to_all | solution.py:451
  496.1 29.3 %attend_back.3 = (bf16[3,1024,768]{2,1,0:T(8,128)(2,1)}, f32[8,768]{1,0:T(8,128)}) custom-call(s32[1]{0:T(128)} %bitcast.25.len_ref, bf16[1024,2304]{1,0:T(8,128)(2,1)} %add_convert_fusion.2.q_ref.k_ref.v_ref, bf16[1024,2304]{1,0:T(8,128)(2,1)} %add_convert_fusion.2.q_ref.k_ref.v_ref, bf16[1024,2304]{1,0:T(8,128)(2,1)} %add_convert_fusion.2.q_ref.k_ref.v_ref, ...), custom_call_target="tpu_custom_call" | custom-call | flops 30000001024 | bytes 15728640 | tf_op jit(solution)/shard_map/attend_back/pallas_call | solution.py:198
  525.5 8.3 %tokens_back.3 = bf16[1024,768]{1,0:T(8,128)(2,1)} custom-call(bf16[3,1024,768]{2,1,0:T(8,128)(2,1)} %get-tuple-element.56.d_ref, bf16[1024,768]{1,0:T(8,128)(2,1)} %get-tuple-element.57.h_ref, bf16[768,2304]{1,0:T(8,128)(2,1)} %bitcast.200), custom_call_target="tpu_custom_call" | custom-call | flops 4000000000 | bytes 12582912 | tf_op jit(solution)/shard_map/tokens_back/pallas_call | solution.py:344
  533.7 12.4 %all-to-all-done.3 = bf16[32,32,768]{2,1,0:T(8,128)(2,1)} async-done(((bf16[32,32,768]{2,1,0:T(8,128)(2,1)}), bf16[32,32,768]{2,1,0:T(8,128)(2,1)}, u32[]{:S(2)}, u32[]{:S(2)}) %all-to-all-start.3) | async-done | bytes 1572896 | tf_op jit(solution)/shard_map/all_to_all | solution.py:429
  546.2 8.1 %all-to-all-start.5 = ((bf16[32,32,768]{2,1,0:T(8,128)(2,1)}), bf16[32,32,768]{2,1,0:T(8,128)(2,1)}, u32[]{:S(2)}, u32[]{:S(2)}) async-start(bf16[32,32,768]{2,1,0:T(8,128)(2,1)} %bitcast.210), calls=%async_computation.5 | async-start | bytes 3145728 | tf_op jit(solution)/shard_map/all_to_all | solution.py:451
  578.7 20.1 %concatenate.40 = bf16[8,4,80,768]{3,2,1,0:T(8,128)(2,1)} concatenate(bf16[8,4,24,768]{3,2,1,0:T(8,128)(2,1)} %bitcast.193, bf16[8,4,24,768]{3,2,1,0:T(8,128)(2,1)} %bitcast.192, bf16[8,4,24,768]{3,2,1,0:T(8,128)(2,1)} %bitcast.191, bf16[8,4,3,768]{3,2,1,0:T(4,128)(2,1)} %broadcast_in_dim.46, bf16[8,4,5,768]{3,2,1,0:T(8,128)(2,1)S(1)} %broadcast_in_dim.47), dimensions={2} | concatenate | bytes 7864320 | tf_op jit(solution)/shard_map/concatenate | solution.py:465
  598.8 6.1 all-to-all-start.6
  624.0 66.9 %all-to-all-done.6 = bf16[32,80,768]{2,1,0:T(8,128)(2,1)} async-done(((bf16[32,80,768]{2,1,0:T(8,128)(2,1)}), bf16[32,80,768]{2,1,0:T(8,128)(2,1)}, u32[]{:S(2)}, u32[]{:S(2)}) %all-to-all-start.6) | async-done | bytes 3932192 | tf_op jit(solution)/shard_map/all_to_all | solution.py:466
  693.6 12.3 %all-gather.2 = bf16[640,768]{1,0:T(8,128)(2,1)S(1)} all-gather(bf16[80,768]{1,0:T(8,128)(2,1)S(1)} %reduce_sum.12), channel_id=4, replica_groups=mesh['rep'=8,'shard'=4] {'rep'}, dimensions={0}, use_global_device_ids=true | all-gather | bytes 1105920 | tf_op jit(solution)/shard_map/all_gather | solution.py:468
  (216 shorter events, 169.1 us)
Async XLA Ops:
  7.2 15.3 %copy-start.11 = (s32[2,32]{1,0:T(2,128)S(1)}, s32[2,32]{1,0:T(2,128)}, u32[]{:S(2)}) copy-start(s32[2,32]{1,0:T(2,128)} %param.23) | copy-start | bytes 772
  7.2 93.1 %all-gather.8.cloned.1.call-start = ((), (), s32[]{:S(2)}) async-start(), calls=%async_computation.9 | async-start | bytes 4055040 | tf_op jit(solution)/shard_map/all_gather | solution.py:403
  16.9 175.7 %all-gather.10.cloned.1.call-start = ((), (), s32[]{:S(2)}) async-start(), calls=%async_computation.10 | async-start | bytes 10948608 | tf_op jit(solution)/shard_map/all_gather | solution.py:411
  29.2 59.4 %all-to-all-start.2 = ((bf16[32,32,768]{2,1,0:T(8,128)(2,1)}), bf16[32,32,768]{2,1,0:T(8,128)(2,1)}, u32[]{:S(2)}, u32[]{:S(2)}) async-start(bf16[32,32,768]{2,1,0:T(8,128)(2,1)} %broadcast_select_fusion), calls=%async_computation.2 | async-start | bytes 3145728 | tf_op jit(solution)/shard_map/all_to_all | solution.py:392
  88.6 9.8 %copy-start.4 = (bf16[2,1,1024,768]{3,2,1,0:T(8,128)(2,1)S(1)}, bf16[2,1,1024,768]{3,2,1,0:T(8,128)(2,1)}, u32[]{:S(2)}) copy-start(bf16[2,1,1024,768]{3,2,1,0:T(8,128)(2,1)} %param.21) | copy-start | bytes 9437188
  88.6 57.9 %all-to-all-start = ((bf16[32,32,768]{2,1,0:T(8,128)(2,1)}), bf16[32,32,768]{2,1,0:T(8,128)(2,1)}, u32[]{:S(2)}, u32[]{:S(2)}) async-start(bf16[32,32,768]{2,1,0:T(8,128)(2,1)} %broadcast_select_fusion.1), calls=%async_computation | async-start | bytes 3145728 | tf_op jit(solution)/shard_map/all_to_all | solution.py:392
  116.0 30.5 %copy-start.3 = (bf16[96,8,3,768]{3,1,2,0:T(8,128)(2,1)}, bf16[96,8,3,768]{3,1,2,0:T(8,128)(2,1)S(1)}, u32[]{:S(2)}) copy-start(bf16[96,8,3,768]{3,1,2,0:T(8,128)(2,1)S(1)} %copy.76) | copy-start | bytes 10616836
  251.8 34.2 %copy-start.15 = (bf16[1024,768]{1,0:T(8,128)(2,1)S(1)}, bf16[1024,768]{1,0:T(8,128)(2,1)}, u32[]{:S(2)}) copy-start(bf16[1024,768]{1,0:T(8,128)(2,1)} %get-tuple-element.44.c_ref) | copy-start | bytes 4718596
  251.8 144.2 %all-to-all-start.1 = ((bf16[32,32,768]{2,1,0:T(8,128)(2,1)}), bf16[32,32,768]{2,1,0:T(8,128)(2,1)S(1)}, u32[]{:S(2)}, u32[]{:S(2)}) async-start(bf16[32,32,768]{2,1,0:T(8,128)(2,1)} %bitcast.209), calls=%async_computation.1 | async-start | bytes 3145728 | tf_op jit(solution)/shard_map/all_to_all | solution.py:429
  285.9 319.3 %reduce-scatter.2.cloned.1.call-start = ((), (), s32[]{:S(2)}) async-start(), calls=%async_computation.8 | async-start | bytes 10948608 | tf_op jit(solution)/shard_map/reduce_scatter | solution.py:440
  290.2 43.1 %copy-start.16 = (bf16[1024,768]{1,0:T(8,128)(2,1)S(1)}, bf16[1024,768]{1,0:T(8,128)(2,1)}, u32[]{:S(2)}) copy-start(bf16[1024,768]{1,0:T(8,128)(2,1)} %get-tuple-element.47.c_ref) | copy-start | bytes 4718596
  338.1 8.6 %slice-start = ((s8[6291456]{0:T(1024)(128)(4,1)}), s8[4194304]{0:T(1024)(128)(4,1)S(1)}, s32[]{:S(2)}) async-start(s8[6291456]{0:T(1024)(128)(4,1)} %bitcast.183), calls=%async_computation.12 | async-start | bytes 8388608
  338.8 8.0 %slice-start.1 = ((s8[6291456]{0:T(1024)(128)(4,1)}), s8[2097152]{0:T(1024)(128)(4,1)S(1)}, s32[]{:S(2)}) async-start(s8[6291456]{0:T(1024)(128)(4,1)} %bitcast.183), calls=%async_computation.13 | async-start | bytes 4194304
  338.8 8.0 %copy-start.5 = (bf16[1024,768]{1,0:T(8,128)(2,1)S(1)}, bf16[1024,768]{1,0:T(8,128)(2,1)}, u32[]{:S(2)}) copy-start(bf16[1024,768]{1,0:T(8,128)(2,1)} %get-tuple-element.66) | copy-start | bytes 4718596
  356.5 9.1 %slice-start.6 = ((s8[6291456]{0:T(1024)(128)(4,1)}), s8[4194304]{0:T(1024)(128)(4,1)S(1)}, s32[]{:S(2)}) async-start(s8[6291456]{0:T(1024)(128)(4,1)} %bitcast.233), calls=%async_computation.18 | async-start | bytes 8388608
  357.7 7.9 %copy-start.17 = (bf16[1024,768]{1,0:T(8,128)(2,1)S(1)}, bf16[1024,768]{1,0:T(8,128)(2,1)}, u32[]{:S(2)}) copy-start(bf16[1024,768]{1,0:T(8,128)(2,1)} %get-tuple-element.71) | copy-start | bytes 4718596
  396.0 37.1 %copy-start.8 = (f32[8,768]{1,0:T(8,128)S(1)}, f32[8,768]{1,0:T(8,128)}, u32[]{:S(2)}) copy-start(f32[8,768]{1,0:T(8,128)} %get-tuple-element.60) | copy-start | bytes 73732
  396.0 37.1 %copy-start.9 = (f32[8,768]{1,0:T(8,128)S(1)}, f32[8,768]{1,0:T(8,128)}, u32[]{:S(2)}) copy-start(f32[8,768]{1,0:T(8,128)} %get-tuple-element.61) | copy-start | bytes 73732
  396.0 96.2 %all-to-all-start.4 = ((bf16[32,32,768]{2,1,0:T(8,128)(2,1)}), bf16[32,32,768]{2,1,0:T(8,128)(2,1)S(1)}, u32[]{:S(2)}, u32[]{:S(2)}) async-start(bf16[32,32,768]{2,1,0:T(8,128)(2,1)} %bitcast.211), calls=%async_computation.4 | async-start | bytes 3145728 | tf_op jit(solution)/shard_map/all_to_all | solution.py:451
  492.1 54.0 %all-to-all-start.3 = ((bf16[32,32,768]{2,1,0:T(8,128)(2,1)}), bf16[32,32,768]{2,1,0:T(8,128)(2,1)}, u32[]{:S(2)}, u32[]{:S(2)}) async-start(bf16[32,32,768]{2,1,0:T(8,128)(2,1)} %bitcast.208), calls=%async_computation.3 | async-start | bytes 3145728 | tf_op jit(solution)/shard_map/all_to_all | solution.py:429
  546.2 52.7 %all-to-all-start.5 = ((bf16[32,32,768]{2,1,0:T(8,128)(2,1)}), bf16[32,32,768]{2,1,0:T(8,128)(2,1)}, u32[]{:S(2)}, u32[]{:S(2)}) async-start(bf16[32,32,768]{2,1,0:T(8,128)(2,1)} %bitcast.210), calls=%async_computation.5 | async-start | bytes 3145728 | tf_op jit(solution)/shard_map/all_to_all | solution.py:451
  555.3 8.2 %slice-start.2 = ((s8[4718592]{0:T(1024)(128)(4,1)}), s8[4194304]{0:T(1024)(128)(4,1)S(1)}, s32[]{:S(2)}) async-start(s8[4718592]{0:T(1024)(128)(4,1)} %bitcast.229), calls=%async_computation.14 | async-start | bytes 8388608
  598.8 92.0 %all-to-all-start.6 = ((bf16[32,80,768]{2,1,0:T(8,128)(2,1)}), bf16[32,80,768]{2,1,0:T(8,128)(2,1)}, u32[]{:S(2)}, u32[]{:S(2)}) async-start(bf16[32,80,768]{2,1,0:T(8,128)(2,1)} %bitcast.177), calls=%async_computation.6 | async-start | bytes 7864320 | tf_op jit(solution)/shard_map/all_to_all | solution.py:466
  604.9 104.9 %all-gather.12.cloned.1.call-start = ((), (), s32[]{:S(2)}) async-start(), calls=%async_computation.11 | async-start | bytes 2985984 | tf_op jit(solution)/shard_map/all_gather | solution.py:441
  (14 other events, 42.6 us)
Sparse Core Ops, SparseCore 0:
  17.0 73.0 all-gather.7
  93.5 99.0 all-gather.9
  374.3 190.2 reduce-scatter.1
  607.3 53.0 all-gather.11
